TPU v7x, 32 devices: a whole 2x2x4 slice. The times are simulated.
32 devices in a mesh: head: 4 (over y, x), seq: 8 (over z, core).
Axes of the slice: x: 2, y: 2, z: 4, core: 2. Of those that a mesh axis runs over, the one named last changes fastest.
Arguments:
- tokens: float32 [8, 1024, 1024], P('seq', 'head'), may hold values from -6 to 6
- patch_counts: int32 [8], P('seq'), may hold values from 256 to 874, as said below
- w_qkv: bfloat16 [1024, 3072], P(('head', 'seq')), may hold values from -0.1875 to 0.1875
- w_out: bfloat16 [1024, 1024], P(('head', 'seq')), may hold values from -3.453125 to 3.453125
- w_up: bfloat16 [1024, 4096], P(('head', 'seq')), may hold values from -0.1875 to 0.1875
- w_down: bfloat16 [4096, 1024], P(('head', 'seq')), may hold values from -0.09375 to 0.09375
- w_patch: bfloat16 [1024, 1024], P(('head', 'seq')), may hold values from -0.1875 to 0.1875
- w_class: bfloat16 [1024, 1024], P(('head', 'seq')), may hold values from -0.1875 to 0.1875
- norm_gains: bfloat16 [2, 1024], P(None, ('head', 'seq')), may hold values from 0.099609375 to 1.8984375
- mask_norm: float32 [2, 150], replicated, may hold values from 0.5 to 1.5
- grad_masks: float32 [8, 1024, 150], P('seq', 'head'), may hold values from -6 to 6
Outputs:
- class_masks: float32 [8, 1024, 150], P('seq', 'head')
- grad_tokens: float32 [8, 1024, 1024], P('seq', 'head')
- grad_w_qkv: float32 [1024, 3072], P(('head', 'seq'))
- grad_w_out: float32 [1024, 1024], P(('head', 'seq'))
- grad_w_up: float32 [1024, 4096], P(('head', 'seq'))
- grad_w_down: float32 [4096, 1024], P(('head', 'seq'))
- grad_w_patch: float32 [1024, 1024], P(('head', 'seq'))
- grad_w_class: float32 [1024, 1024], P(('head', 'seq'))
- grad_norm_gains: float32 [2, 1024], P(None, ('head', 'seq'))
- grad_mask_norm: float32 [2, 150], replicated
Inputs may be any that keep to these rules, and one draw needn't show every extreme that they name: An image's slot holds its 150 class rows first, then patch_counts[i] patch rows, then padding; some image has 874 patches and some 1024 // 4.
All inputs are finite; a program needn't handle non-finite values.
Results may differ from a plain program's by a relative error of at most 0.02.
Values may be sent and summed in bfloat16 or wider, within the bound.
A program may use at most 192 MiB of HBM per device.

v0:
```python
from functools import partial

import jax
import jax.numpy as jnp
from jax import lax
from jax.sharding import PartitionSpec as P

HEADS = 16
DH = 64
CLS = 150


def spread_2(value, axis, source):
    kept = jnp.where(lax.axis_index(axis) == source, value, 0).astype(value.dtype)
    return lax.psum(kept, axis)


def standardize(values):
    center = values - jnp.mean(values, axis=-1, keepdims=True)
    inverse = lax.rsqrt(jnp.mean(center * center, axis=-1, keepdims=True) + 1e-05)
    return (center * inverse, inverse)


def standard_back(normal, inverse, upstream):
    middle = jnp.mean(upstream, axis=-1, keepdims=True)
    along = jnp.mean(upstream * normal, axis=-1, keepdims=True)
    return inverse * (upstream - middle - normal * along)


def unit_scale(values):
    return lax.rsqrt(jnp.sum(values * values, axis=-1, keepdims=True) + 1e-06)


def unit_back(values, upstream):
    factor = unit_scale(values)
    direct = values * factor
    return factor * (upstream - direct * jnp.sum(upstream * direct, axis=-1, keepdims=True))


def block_scores(query_block, key_rows, key_live, scaling):
    scores = (
        jnp.einsum("qd,kd->qk", query_block, key_rows, preferred_element_type=jnp.float32) * scaling
    )
    return jnp.where(key_live, scores, -1e30)


def attend_head(queries, key_rows, values, key_live, scaling, blocks):
    head_width = queries.shape[-1]

    def single(query_block):
        scores = block_scores(query_block, key_rows, key_live, scaling)
        highest = jnp.max(scores, axis=-1, keepdims=True)
        weights_raw = jnp.exp(scores - highest)
        totals = jnp.sum(weights_raw, axis=-1, keepdims=True)
        weights = (weights_raw / totals).astype(jnp.bfloat16)
        output = jnp.einsum("qk,kd->qd", weights, values, preferred_element_type=jnp.float32)
        return (output.astype(jnp.bfloat16), (highest + jnp.log(totals))[:, 0])

    outputs, logsum = lax.map(single, queries.reshape(blocks, -1, head_width))
    return (outputs.reshape(-1, head_width), logsum.reshape(-1))


def attend_back(queries, key_rows, values, grad_out, logsum, key_live, scaling, blocks):
    head_width = queries.shape[-1]

    def single(running, pieces):
        grad_keys, grad_values = running
        query_block, grad_block, logsum_block = pieces
        scores = block_scores(query_block, key_rows, key_live, scaling)
        weights = jnp.exp(scores - logsum_block[:, None])
        grad_values = grad_values + jnp.einsum(
            "qk,qd->kd",
            weights.astype(jnp.bfloat16),
            grad_block,
            preferred_element_type=jnp.float32,
        )
        grad_weights = jnp.einsum(
            "qd,kd->qk", grad_block, values, preferred_element_type=jnp.float32
        )
        deltas = jnp.sum(grad_weights * weights, axis=-1, keepdims=True)
        grad_scores = (weights * (grad_weights - deltas)).astype(jnp.bfloat16)
        grad_query = (
            jnp.einsum("qk,kd->qd", grad_scores, key_rows, preferred_element_type=jnp.float32)
            * scaling
        )
        grad_keys = (
            grad_keys
            + jnp.einsum("qk,qd->kd", grad_scores, query_block, preferred_element_type=jnp.float32)
            * scaling
        )
        return ((grad_keys, grad_values), grad_query)

    zero_state = jnp.zeros(key_rows.shape, jnp.float32)
    pieces = (
        queries.reshape(blocks, -1, head_width),
        grad_out.reshape(blocks, -1, head_width),
        logsum.reshape(blocks, -1),
    )
    (grad_keys, grad_values), grad_queries = lax.scan(single, (zero_state, zero_state), pieces)
    return (grad_queries.reshape(-1, head_width), grad_keys, grad_values)


def body(
    tokens,
    patch_counts,
    w_qkv,
    w_out,
    w_up,
    w_down,
    w_patch,
    w_class,
    norm_gains,
    mask_norm,
    grad_masks,
):
    gains_rows = norm_gains.T
    gathered = (
        lax.all_gather(w_qkv, ("head", "seq"), axis=0, tiled=True),
        lax.all_gather(w_out, ("head", "seq"), axis=0, tiled=True),
        lax.all_gather(w_up, ("head", "seq"), axis=0, tiled=True),
        lax.all_gather(w_down, ("head", "seq"), axis=0, tiled=True),
        lax.all_gather(w_patch, ("head", "seq"), axis=0, tiled=True),
        lax.all_gather(w_class, ("head", "seq"), axis=0, tiled=True),
        lax.all_gather(gains_rows, ("head", "seq"), axis=0, tiled=True),
    )
    full_qkv, full_out, full_up, full_down, full_patch, full_class, full_gains = gathered
    gain_one = full_gains[:, 0].astype(jnp.float32)
    gain_two = full_gains[:, 1].astype(jnp.float32)
    image_count = tokens.shape[0]
    row_count = tokens.shape[1]
    groups = lax.axis_size("head")
    slot_rows = row_count * groups
    local_heads = HEADS // groups
    position = lax.axis_index("head") * row_count + jnp.arange(row_count, dtype=jnp.int32)
    live_limit = CLS + patch_counts
    patch_rows = ((position[None, :] >= CLS) & (position[None, :] < live_limit[:, None])).astype(
        jnp.float32
    )[:, :, None]
    key_live = (jnp.arange(slot_rows, dtype=jnp.int32)[None, :] < live_limit[:, None])[:, None, :]
    root_flag = (lax.axis_index("head") == 0).astype(jnp.float32)
    scaling = DH ** (-0.5)
    blocks = slot_rows // 512
    normal_one, inverse_one = standardize(tokens)
    normed_one = (normal_one * gain_one).astype(jnp.bfloat16)
    triple = jnp.einsum(
        "ird,dt->irt", normed_one, full_qkv, preferred_element_type=jnp.float32
    ).astype(jnp.bfloat16)
    spread = lax.all_to_all(triple, "head", split_axis=2, concat_axis=1, tiled=True).reshape(
        image_count, slot_rows, local_heads, 3, DH
    )
    image = 0
    outputs = []
    image_logsums = []
    for number in range(local_heads):
        output, logsum = attend_head(
            spread[image, :, number, 0],
            spread[image, :, number, 1],
            spread[image, :, number, 2],
            key_live[image],
            scaling,
            blocks,
        )
        outputs.append(output)
        image_logsums.append(logsum)
    image_outputs = [jnp.stack(outputs, axis=1).reshape(slot_rows, local_heads * DH)]
    logsums = [image_logsums]
    attended_heads = jnp.stack(image_outputs, axis=0)
    attended = lax.all_to_all(attended_heads, "head", split_axis=1, concat_axis=2, tiled=True)
    second = tokens + jnp.einsum(
        "ire,ed->ird", attended, full_out, preferred_element_type=jnp.float32
    )
    normal_two, inverse_two = standardize(second)
    normed_two = (normal_two * gain_two).astype(jnp.bfloat16)
    hidden = jnp.einsum("ird,df->irf", normed_two, full_up, preferred_element_type=jnp.float32)
    gelu_exact = partial(jax.nn.gelu, approximate=False)
    active = gelu_exact(hidden).astype(jnp.bfloat16)
    residual = second + jnp.einsum(
        "irf,fd->ird", active, full_down, preferred_element_type=jnp.float32
    )
    rounded = residual.astype(jnp.bfloat16)
    patch_proj = jnp.einsum("ird,de->ire", rounded, full_patch, preferred_element_type=jnp.float32)
    patch_unit = (patch_proj * unit_scale(patch_proj)).astype(jnp.bfloat16)
    class_proj = jnp.einsum(
        "ird,de->ire", rounded[:, :CLS], full_class, preferred_element_type=jnp.float32
    )
    class_unit = (class_proj * unit_scale(class_proj)).astype(jnp.bfloat16)
    classes = spread_2(class_unit, "head", 0)
    products = jnp.einsum("ird,icd->irc", patch_unit, classes, preferred_element_type=jnp.float32)
    normal_mask, inverse_mask = standardize(products)
    class_masks = (normal_mask * mask_norm[0] + mask_norm[1]) * patch_rows
    upstream = grad_masks * patch_rows
    norm_grads = lax.psum(
        jnp.stack([jnp.sum(upstream * normal_mask, axis=(0, 1)), jnp.sum(upstream, axis=(0, 1))]),
        ("head", "seq"),
    )
    d_products = standard_back(normal_mask, inverse_mask, upstream * mask_norm[0]).astype(
        jnp.bfloat16
    )
    d_patch_unit = jnp.einsum(
        "irc,icd->ird", d_products, classes, preferred_element_type=jnp.float32
    )
    class_part = jnp.einsum(
        "irc,ird->icd", d_products, patch_unit, preferred_element_type=jnp.float32
    )
    d_class_unit = lax.psum(class_part.astype(jnp.bfloat16), "head").astype(jnp.float32)
    d_patch_proj = unit_back(patch_proj, d_patch_unit).astype(jnp.bfloat16)
    d_class_proj = (unit_back(class_proj, d_class_unit) * root_flag).astype(jnp.bfloat16)
    regathered = (
        lax.all_gather(w_qkv, ("head", "seq"), axis=0, tiled=True),
        lax.all_gather(w_out, ("head", "seq"), axis=0, tiled=True),
        lax.all_gather(w_up, ("head", "seq"), axis=0, tiled=True),
        lax.all_gather(w_down, ("head", "seq"), axis=0, tiled=True),
        lax.all_gather(w_patch, ("head", "seq"), axis=0, tiled=True),
        lax.all_gather(w_class, ("head", "seq"), axis=0, tiled=True),
        lax.all_gather(gains_rows, ("head", "seq"), axis=0, tiled=True),
    )
    back_qkv, back_out, back_up, back_down, back_patch, back_class, back_gains = regathered
    back_one = back_gains[:, 0].astype(jnp.float32)
    back_two = back_gains[:, 1].astype(jnp.float32)
    grad_patch = jnp.einsum(
        "ird,ire->de", rounded, d_patch_proj, preferred_element_type=jnp.float32
    )
    grad_class = jnp.einsum(
        "ird,ire->de", rounded[:, :CLS], d_class_proj, preferred_element_type=jnp.float32
    )
    d_residual = jnp.einsum(
        "ire,de->ird", d_patch_proj, back_patch, preferred_element_type=jnp.float32
    )
    class_term = jnp.einsum(
        "ire,de->ird", d_class_proj, back_class, preferred_element_type=jnp.float32
    )
    d_residual = d_residual.at[:, :CLS].add(class_term)
    d_branch = d_residual.astype(jnp.bfloat16)
    grad_down = jnp.einsum("irf,ird->fd", active, d_branch, preferred_element_type=jnp.float32)
    d_active = jnp.einsum("ird,fd->irf", d_branch, back_down, preferred_element_type=jnp.float32)
    gelu_pull = jax.vjp(gelu_exact, hidden)[1]
    d_hidden = gelu_pull(d_active)[0].astype(jnp.bfloat16)
    grad_up = jnp.einsum("ird,irf->df", normed_two, d_hidden, preferred_element_type=jnp.float32)
    d_normed_two = jnp.einsum("irf,df->ird", d_hidden, back_up, preferred_element_type=jnp.float32)
    d_second = d_residual + standard_back(normal_two, inverse_two, d_normed_two * back_two)
    grad_gain_two = jnp.sum(d_normed_two * normal_two, axis=(0, 1))
    d_mix = d_second.astype(jnp.bfloat16)
    grad_out = jnp.einsum("ire,ird->ed", attended, d_mix, preferred_element_type=jnp.float32)
    d_attended = jnp.einsum(
        "ird,ed->ire", d_mix, back_out, preferred_element_type=jnp.float32
    ).astype(jnp.bfloat16)
    d_heads = lax.all_to_all(d_attended, "head", split_axis=2, concat_axis=1, tiled=True).reshape(
        image_count, slot_rows, local_heads, DH
    )
    image = 0
    head_grads = []
    for number in range(local_heads):
        grad_queries, grad_keys, grad_values = attend_back(
            spread[image, :, number, 0],
            spread[image, :, number, 1],
            spread[image, :, number, 2],
            d_heads[image, :, number],
            logsums[image][number],
            key_live[image],
            scaling,
            blocks,
        )
        head_grads.append(jnp.stack([grad_queries, grad_keys, grad_values], axis=1))
    image_grads = [jnp.stack(head_grads, axis=1).reshape(slot_rows, local_heads * 3 * DH)]
    d_spread = jnp.stack(image_grads, axis=0).astype(jnp.bfloat16)
    d_triple = lax.all_to_all(d_spread, "head", split_axis=1, concat_axis=2, tiled=True)
    grad_qkv = jnp.einsum("ird,irt->dt", normed_one, d_triple, preferred_element_type=jnp.float32)
    d_normed_one = jnp.einsum("irt,dt->ird", d_triple, back_qkv, preferred_element_type=jnp.float32)
    grad_inputs = d_second + standard_back(normal_one, inverse_one, d_normed_one * back_one)
    grad_gain_one = jnp.sum(d_normed_one * normal_one, axis=(0, 1))
    grad_gains = jnp.stack([grad_gain_one, grad_gain_two], axis=1)
    reduced = (
        lax.psum_scatter(grad_qkv, ("head", "seq"), scatter_dimension=0, tiled=True),
        lax.psum_scatter(grad_out, ("head", "seq"), scatter_dimension=0, tiled=True),
        lax.psum_scatter(grad_up, ("head", "seq"), scatter_dimension=0, tiled=True),
        lax.psum_scatter(grad_down, ("head", "seq"), scatter_dimension=0, tiled=True),
        lax.psum_scatter(grad_patch, ("head", "seq"), scatter_dimension=0, tiled=True),
        lax.psum_scatter(grad_class, ("head", "seq"), scatter_dimension=0, tiled=True),
        lax.psum_scatter(grad_gains, ("head", "seq"), scatter_dimension=0, tiled=True),
    )
    return (
        class_masks,
        grad_inputs,
        reduced[0],
        reduced[1],
        reduced[2],
        reduced[3],
        reduced[4],
        reduced[5],
        reduced[6].T,
        norm_grads,
    )


def solution(mesh):
    return jax.shard_map(
        body,
        mesh=mesh,
        in_specs=(
            P("seq", "head", None),
            P("seq"),
            P(("head", "seq"), None),
            P(("head", "seq"), None),
            P(("head", "seq"), None),
            P(("head", "seq"), None),
            P(("head", "seq"), None),
            P(("head", "seq"), None),
            P(None, ("head", "seq")),
            P(),
            P("seq", "head", None),
        ),
        out_specs=(
            P("seq", "head", None),
            P("seq", "head", None),
            P(("head", "seq"), None),
            P(("head", "seq"), None),
            P(("head", "seq"), None),
            P(("head", "seq"), None),
            P(("head", "seq"), None),
            P(("head", "seq"), None),
            P(None, ("head", "seq")),
            P(),
        ),
        check_vma=False,
    )
```

profile of v0, /device:TPU:0, one launch (start us, length us, event | category | flops | bytes accessed | tf_op | source)
XLA Modules:
  0.0 1819.9 jit_solution(12584200432137674807)
XLA Ops:
  10.0 43.2 %all-gather = bf16[32,32,2]{1,2,0:T(2,128)(2,1)S(1)} all-gather(bf16[1,32,2]{1,2,0:T(2,128)(2,1)} %bitcast.568), channel_id=1, replica_groups=mesh['head'=4,'seq'=8] {'head','seq'}, dimensions={0}, use_global_device_ids=true | all-gather | bytes 4224 | tf_op jit(solution)/shard_map/all_gather | solution.py:124
  55.0 28.3 %all-gather.8.cloned.1.call-done = bf16[1024,3072]{1,0:T(8,128)(2,1)} async-done(((bf16[32,3072]{1,0:T(8,128)(2,1)}), bf16[1024,3072]{1,0:T(8,128)(2,1)}) %all-gather.8.cloned.1.call-update) | async-done | bytes 6291472 | tf_op jit(solution)/shard_map/all_gather | solution.py:118
  94.0 16.6 reduce.41
  117.3 22.4 %all-to-all-done = bf16[4,2,98304]{2,1,0:T(2,128)(2,1)S(1)} async-done(((bf16[4,2,98304]{2,1,0:T(2,128)(2,1)}), bf16[4,2,98304]{2,1,0:T(2,128)(2,1)S(1)}, u32[]{:S(2)}, u32[]{:S(2)}) %all-to-all-start) | async-done | bytes 1572896 | tf_op jit(solution)/shard_map/all_to_all | solution.py:148
  155.1 7.9 while.116
  200.2 25.5 %all-gather.12.cloned.1.call-done = bf16[1024,4096]{1,0:T(8,128)(2,1)} async-done(((bf16[32,4096]{1,0:T(8,128)(2,1)}), bf16[1024,4096]{1,0:T(8,128)(2,1)}) %all-gather.12.cloned.1.call-update) | async-done | bytes 8388624 | tf_op jit(solution)/shard_map/all_gather | solution.py:120
  225.6 15.6 multiply_convert_fusion.4
  241.3 63.2 %all-gather.14.cloned.1.call-done = bf16[4096,1024]{1,0:T(8,128)(2,1)} async-done(((bf16[128,1024]{1,0:T(8,128)(2,1)}), bf16[4096,1024]{1,0:T(8,128)(2,1)}) %all-gather.14.cloned.1.call-update) | async-done | bytes 8388624 | tf_op jit(solution)/shard_map/all_gather | solution.py:121
  310.9 51.6 %all-gather.18.cloned.1.call-done = bf16[1024,1024]{1,0:T(8,128)(2,1)} async-done(((bf16[32,1024]{1,0:T(8,128)(2,1)}), bf16[1024,1024]{1,0:T(8,128)(2,1)}) %all-gather.18.cloned.1.call-update) | async-done | bytes 2097168 | tf_op jit(solution)/shard_map/all_gather | solution.py:123
  365.8 54.8 %all-gather.16.cloned.1.call-done = bf16[1024,1024]{1,0:T(8,128)(2,1)} async-done(((bf16[32,1024]{1,0:T(8,128)(2,1)}), bf16[1024,1024]{1,0:T(8,128)(2,1)}) %all-gather.16.cloned.1.call-update) | async-done | bytes 2097168 | tf_op jit(solution)/shard_map/all_gather | solution.py:122
  423.2 43.2 %all-reduce.3.cloned.1.call-done = bf16[150,1024]{1,0:T(8,128)(2,1)} async-done(((bf16[150,1024]{1,0:T(8,128)(2,1)}), bf16[150,1024]{1,0:T(8,128)(2,1)}) %all-reduce.3.cloned.1.call-update) | async-done | bytes 307216 | tf_op jit(solution)/shard_map/psum | solution.py:15
  473.3 40.5 %all-reduce.5.cloned.1.call-done = bf16[1,150,1024]{2,1,0:T(8,128)(2,1)} async-done(((bf16[1,150,1024]{2,1,0:T(8,128)(2,1)}), bf16[1,150,1024]{2,1,0:T(8,128)(2,1)}) %all-reduce.5.cloned.1.call-update) | async-done | bytes 307216 | tf_op jit(solution)/shard_map/psum | solution.py:205
  520.6 11.6 add_convert_fusion
  551.4 7.8 all-to-all-done.2
  562.5 17.7 while.120
  587.6 17.2 while.119
  612.2 17.2 while.118
  636.8 16.8 while.117
  659.3 7.6 copy.202
  667.0 11.4 reduce.44
  680.8 22.2 %all_to_all.60 = bf16[4,2,98304]{2,1,0:T(2,128)(2,1)} all-to-all(bf16[4,2,98304]{2,1,0:T(2,128)(2,1)S(1)} %reshape.601), channel_id=1, replica_groups=mesh['head'=4,'seq'=8] {'head'}, dimensions={0} | all-to-all | bytes 3145728 | tf_op jit(solution)/shard_map/all_to_all | solution.py:266
  730.5 7.9 fusion.185
  739.6 9.8 fusion.181
  750.6 9.7 fusion.154
  762.2 39.4 %psum.23 = f32[2,150]{1,0:T(2,128)} all-reduce(f32[2,150]{1,0:T(2,128)S(1)} %pad_maximum_fusion.3), channel_id=1, replica_groups=mesh['head'=4,'seq'=8] {'head','seq'}, use_global_device_ids=true, to_apply=%region_57.58 | all-reduce | flops 300 | bytes 2400 | tf_op jit(solution)/shard_map/psum | solution.py:192
  803.1 47.7 %reduce-scatter.22.cloned.1.call-done = f32[32,2]{1,0:T(8,128)} async-done(((f32[1024,2]{1,0:T(8,128)}), f32[32,2]{1,0:T(8,128)}) %reduce-scatter.22.cloned.1.call-update) | async-done | bytes 272
  852.2 140.6 %reduce-scatter.18.cloned.1.call-done = f32[32,1024]{1,0:T(8,128)} async-done(((f32[1024,1024]{1,0:T(8,128)}), f32[32,1024]{1,0:T(8,128)}) %reduce-scatter.18.cloned.1.call-update) | async-done | bytes 131088 | tf_op jit(solution)/shard_map/reduce_scatter | solution.py:277
  992.8 142.4 %reduce-scatter.12.cloned.1.call-done = f32[32,1024]{1,0:T(8,128)} async-done(((f32[1024,1024]{1,0:T(8,128)}), f32[32,1024]{1,0:T(8,128)}) %reduce-scatter.12.cloned.1.call-update) | async-done | bytes 131088 | tf_op jit(solution)/shard_map/reduce_scatter | solution.py:274
  1135.3 142.3 %reduce-scatter.20.cloned.1.call-done = f32[32,1024]{1,0:T(8,128)} async-done(((f32[1024,1024]{1,0:T(8,128)}), f32[32,1024]{1,0:T(8,128)}) %reduce-scatter.20.cloned.1.call-update) | async-done | bytes 131088 | tf_op jit(solution)/shard_map/reduce_scatter | solution.py:278
  1277.6 160.0 %reduce-scatter.10.cloned.1.call-done = f32[32,3072]{1,0:T(8,128)} async-done(((f32[1024,3072]{1,0:T(8,128)}), f32[32,3072]{1,0:T(8,128)}) %reduce-scatter.10.cloned.1.call-update) | async-done | bytes 393232 | tf_op jit(solution)/shard_map/reduce_scatter | solution.py:273
  1437.5 188.5 %reduce-scatter.14.cloned.1.call-done = f32[32,4096]{1,0:T(8,128)} async-done(((f32[1024,4096]{1,0:T(8,128)}), f32[32,4096]{1,0:T(8,128)}) %reduce-scatter.14.cloned.1.call-update) | async-done | bytes 524304 | tf_op jit(solution)/shard_map/reduce_scatter | solution.py:275
  1626.1 187.1 %reduce-scatter.16.cloned.1.call-done = f32[128,1024]{1,0:T(8,128)} async-done(((f32[4096,1024]{1,0:T(8,128)}), f32[128,1024]{1,0:T(8,128)}) %reduce-scatter.16.cloned.1.call-update) | async-done | bytes 524304 | tf_op jit(solution)/shard_map/reduce_scatter | solution.py:276
  (489 shorter events, 273.5 us)
Async XLA Ops:
  7.2 47.5 %copy-start.4 = (f32[1,256,1024]{2,1,0:T(8,128)S(1)}, f32[1,256,1024]{2,1,0:T(8,128)}, u32[]{:S(2)}) copy-start(f32[1,256,1024]{2,1,0:T(8,128)} %param.29) | copy-start | bytes 3145732
  7.2 76.1 %all-gather.8.cloned.1.call-start = ((), (), s32[]{:S(2)}) async-start(), calls=%async_computation.11 | async-start | bytes 6488064 | tf_op jit(solution)/shard_map/all_gather | solution.py:118
  7.9 189.3 %all-gather.10.cloned.1.call-start = ((), (), s32[]{:S(2)}) async-start(), calls=%async_computation.12 | async-start | bytes 2162688 | tf_op jit(solution)/shard_map/all_gather | solution.py:119
  8.7 217.0 %all-gather.12.cloned.1.call-start = ((), (), s32[]{:S(2)}) async-start(), calls=%async_computation.13 | async-start | bytes 8650752 | tf_op jit(solution)/shard_map/all_gather | solution.py:120
  9.4 295.1 %all-gather.14.cloned.1.call-start = ((), (), s32[]{:S(2)}) async-start(), calls=%async_computation.14 | async-start | bytes 8650752 | tf_op jit(solution)/shard_map/all_gather | solution.py:121
  54.7 33.3 %copy-start.73 = (f32[256]{0:T(256)}, f32[256]{0:T(256)S(1)}, u32[]{:S(2)}) copy-start(f32[256]{0:T(256)S(1)} %broadcast_multiply_fusion.8) | copy-start | bytes 3076
  55.0 484.7 %copy-start.53 = (f32[1024,1]{0,1:T(1,128)}, f32[1024,1]{0,1:T(1,128)S(1)}, u32[]{:S(2)}) copy-start(f32[1024,1]{0,1:T(1,128)S(1)} %get-tuple-element.1122) | copy-start | bytes 12292
  112.5 27.2 %all-to-all-start = ((bf16[4,2,98304]{2,1,0:T(2,128)(2,1)}), bf16[4,2,98304]{2,1,0:T(2,128)(2,1)S(1)}, u32[]{:S(2)}, u32[]{:S(2)}) async-start(bf16[4,2,98304]{2,1,0:T(2,128)(2,1)} %reshape.595), calls=%async_computation | async-start | bytes 3145728 | tf_op jit(solution)/shard_map/all_to_all | solution.py:148
  116.0 246.4 %all-gather.18.cloned.1.call-start = ((), (), s32[]{:S(2)}) async-start(), calls=%async_computation.16 | async-start | bytes 2162688 | tf_op jit(solution)/shard_map/all_gather | solution.py:123
  185.1 11.3 all-to-all-start.1
  188.6 232.1 %all-gather.16.cloned.1.call-start = ((), (), s32[]{:S(2)}) async-start(), calls=%async_computation.15 | async-start | bytes 2162688 | tf_op jit(solution)/shard_map/all_gather | solution.py:122
  189.2 277.3 %all-reduce.3.cloned.1.call-start = ((), (), s32[]{:S(2)}) async-start(), calls=%async_computation.17 | async-start | bytes 622592 | tf_op jit(solution)/shard_map/psum | solution.py:15
  189.2 280.5 %copy-start.67 = (f32[256]{0:T(256)}, f32[256]{0:T(256)S(1)}, u32[]{:S(2)}) copy-start(f32[256]{0:T(256)S(1)} %and_convert_fusion) | copy-start | bytes 3076
  189.8 280.0 %copy-start.69 = (f32[1,150]{1,0:T(1,128)}, f32[1,150]{1,0:T(1,128)S(1)}, u32[]{:S(2)}) copy-start(f32[1,150]{1,0:T(1,128)S(1)} %get-tuple-element.1124) | copy-start | bytes 1804
  199.9 339.9 %copy-start.6 = (f32[1,256,1024]{2,1,0:T(8,128)}, f32[1,256,1024]{2,1,0:T(8,128)S(1)}, u32[]{:S(2)}) copy-start(f32[1,256,1024]{2,1,0:T(8,128)S(1)} %get-tuple-element.1127) | copy-start | bytes 3145732
  199.9 339.9 %copy-start.65 = (f32[256]{0:T(256)}, f32[256]{0:T(256)S(1)}, u32[]{:S(2)}) copy-start(f32[256]{0:T(256)S(1)} %broadcast_multiply_fusion.7) | copy-start | bytes 3076
  200.2 339.6 %copy-start.71 = (f32[256]{0:T(256)}, f32[256]{0:T(256)S(1)}, u32[]{:S(2)}) copy-start(f32[256]{0:T(256)S(1)} %add_rsqrt_fusion.3) | copy-start | bytes 3076
  310.9 54.7 %copy-start.25 = (bf16[1,256,1024]{2,1,0:T(8,128)(2,1)}, bf16[1,256,1024]{2,1,0:T(8,128)(2,1)S(1)}, u32[]{:S(2)}) copy-start(bf16[1,256,1024]{2,1,0:T(8,128)(2,1)S(1)} %fusion.133) | copy-start | bytes 1572868
  364.6 150.4 %copy-start.10 = (f32[150,1024]{1,0:T(8,128)}, f32[150,1024]{1,0:T(8,128)S(1)}, u32[]{:S(2)}) copy-start(f32[150,1024]{1,0:T(8,128)S(1)} %get-tuple-element.1130) | copy-start | bytes 1843204
  364.7 150.3 %copy-start.62 = (f32[150]{0:T(256)}, f32[150]{0:T(256)S(1)}, u32[]{:S(2)}) copy-start(f32[150]{0:T(256)S(1)} %add_rsqrt_fusion.1) | copy-start | bytes 1804
  365.6 102.3 %copy-start.36 = (f32[1,256,150]{1,0,2:T(1,128)S(1)}, f32[1,256,150]{1,0,2:T(1,128)}, u32[]{:S(2)}) copy-start(f32[1,256,150]{1,0,2:T(1,128)} %param.39) | copy-start | bytes 460804
  365.6 148.2 %all-reduce.5.cloned.1.call-start = ((), (), s32[]{:S(2)}) async-start(), calls=%async_computation.18 | async-start | bytes 622592 | tf_op jit(solution)/shard_map/psum | solution.py:205
  547.8 11.4 all-to-all-start.2
  551.3 299.6 %reduce-scatter.22.cloned.1.call-start = ((), (), s32[]{:S(2)}) async-start(), calls=%async_computation.25 | async-start | bytes 540672
  717.2 275.7 %reduce-scatter.18.cloned.1.call-start = ((), (), s32[]{:S(2)}) async-start(), calls=%async_computation.23 | async-start | bytes 4325376 | tf_op jit(solution)/shard_map/reduce_scatter | solution.py:277
  721.0 414.3 %reduce-scatter.12.cloned.1.call-start = ((), (), s32[]{:S(2)}) async-start(), calls=%async_computation.20 | async-start | bytes 4325376 | tf_op jit(solution)/shard_map/reduce_scatter | solution.py:274
  725.1 552.5 %reduce-scatter.20.cloned.1.call-start = ((), (), s32[]{:S(2)}) async-start(), calls=%async_computation.24 | async-start | bytes 4325376 | tf_op jit(solution)/shard_map/reduce_scatter | solution.py:278
  729.8 707.7 %reduce-scatter.10.cloned.1.call-start = ((), (), s32[]{:S(2)}) async-start(), calls=%async_computation.19 | async-start | bytes 12976128 | tf_op jit(solution)/shard_map/reduce_scatter | solution.py:273
  738.4 887.7 %reduce-scatter.14.cloned.1.call-start = ((), (), s32[]{:S(2)}) async-start(), calls=%async_computation.21 | async-start | bytes 17301504 | tf_op jit(solution)/shard_map/reduce_scatter | solution.py:275
  749.4 1063.7 %reduce-scatter.16.cloned.1.call-start = ((), (), s32[]{:S(2)}) async-start(), calls=%async_computation.22 | async-start | bytes 17301504 | tf_op jit(solution)/shard_map/reduce_scatter | solution.py:276
  760.4 41.2 %copy-start.33 = (f32[256,1024]{1,0:T(8,128)S(1)}, f32[256,1024]{1,0:T(8,128)}, u32[]{:S(2)}) copy-start(f32[256,1024]{1,0:T(8,128)} %get-tuple-element.1138) | copy-start | bytes 3145732
  760.4 41.4 %copy-start.85 = (f32[256]{0:T(256)S(1)}, f32[256]{0:T(256)}, u32[]{:S(2)}) copy-start(f32[256]{0:T(256)} %get-tuple-element.945) | copy-start | bytes 3076
  (83 other events, 319.6 us)
Sparse Core Ops, SparseCore 0:
  11.0 72.2 all-gather.7
  86.3 57.6 all-gather.9
  147.0 78.5 all-gather.11
  228.5 75.9 all-gather.13
  307.3 55.0 all-gather.17
  365.3 55.3 all-gather.15
  424.2 42.2 all-reduce.2
  470.3 43.4 all-reduce.4
  717.3 133.5 reduce-scatter.21
  853.7 139.1 reduce-scatter.17
  995.8 139.4 reduce-scatter.11
  1138.1 139.4 reduce-scatter.19
  1285.2 152.2 reduce-scatter.9
  1440.3 185.7 reduce-scatter.13
  1628.8 184.3 reduce-scatter.15
where the time goes:
time: 1830 us; the launch traced here: 1820 us
  waiting for transfers between devices  1360 us (74%)
  matrix products  182 us (10%)
  blocking collectives  105 us (6%)
  local copies, waits for them, and re-layouts  84.2 us (5%)
  other arithmetic  63.8 us (3%)
    reduce_scatter x1, waiting for transfers between devices, body(): lax.psum_scatter(grad_up, ('head', 'seq'), scatter_dimension=0, tiled=True)  189 us
    reduce_scatter x1, waiting for transfers between devices, body(): lax.psum_scatter(grad_down, ('head', 'seq'), scatter_dimension=0, tiled=T...  187 us
    reduce_scatter x1, waiting for transfers between devices, body(): lax.psum_scatter(grad_qkv, ('head', 'seq'), scatter_dimension=0, tiled=True)  160 us
    reduce_scatter x1, waiting for transfers between devices, body(): lax.psum_scatter(grad_out, ('head', 'seq'), scatter_dimension=0, tiled=True)  142 us
    reduce_scatter x1, waiting for transfers between devices, body(): lax.psum_scatter(grad_class, ('head', 'seq'), scatter_dimension=0, tiled=...  142 us
    reduce_scatter x1, waiting for transfers between devices, body(): lax.psum_scatter(grad_patch, ('head', 'seq'), scatter_dimension=0, tiled=...  141 us
    all_gather x1, waiting for transfers between devices, body(): lax.all_gather(w_down, ('head', 'seq'), axis=0, tiled=True)  63.2 us
    all_gather x1, waiting for transfers between devices, body(): lax.all_gather(w_patch, ('head', 'seq'), axis=0, tiled=True)  54.8 us
  transfers between devices with their start and end apart: 18, of which 17 were waited for; matrix products, arithmetic and copies ran while one was open for 8% of the time, Pallas kernels for 0%

commit v1 on v0

--- a/solution.py
+++ b/solution.py
@@ -3,6 +3,8 @@
 import jax
 import jax.numpy as jnp
 from jax import lax
+from jax.experimental import pallas as pl
+from jax.experimental.pallas import tpu as pltpu
 from jax.sharding import PartitionSpec as P
 
 HEADS = 16
@@ -100,7 +102,7 @@
     return (grad_queries.reshape(-1, head_width), grad_keys, grad_values)
 
 
-def body(
+def body_general(
     tokens,
     patch_counts,
     w_qkv,
@@ -292,9 +294,712 @@
     )
 
 
+MESH = pl.DeviceIdType.MESH
+LOG2E = 1.4426950408889634
+
+
+def place():
+    h = lax.axis_index("head")
+    s = lax.axis_index("seq")
+    return h // 2, h % 2, s // 2, s % 2
+
+
+def device(y, x, z, c):
+    return (y * 2 + x, z * 2 + c)
+
+
+def greet(peers):
+    barrier = pltpu.get_barrier_semaphore()
+    for peer in peers:
+        pl.semaphore_signal(barrier, inc=1, device_id=peer, device_id_type=MESH)
+    pl.semaphore_wait(barrier, len(peers))
+
+
+class Copies:
+    def __init__(self, send_sem, recv_sem):
+        self.send_sem, self.recv_sem, self.made = send_sem, recv_sem, []
+
+    def start(self, source, target, peer):
+        number = len(self.made)
+        copy = pltpu.make_async_remote_copy(
+            src_ref=source,
+            dst_ref=target,
+            send_sem=self.send_sem.at[number],
+            recv_sem=self.recv_sem.at[number],
+            device_id=peer,
+            device_id_type=MESH,
+        )
+        copy.start()
+        self.made.append(copy)
+        return copy
+
+    def drain(self):
+        for copy in self.made:
+            copy.wait_send()
+
+
+def gather_kernel(names, *refs):
+    count = len(names)
+    shards, fulls = refs[:count], refs[count : 2 * count]
+    send_sem, recv_sem, local_sem = refs[2 * count :]
+    y, x, z, c = place()
+    sibling, x_peer, y_peer = device(y, x, z, 1 - c), device(y, 1 - x, z, c), device(1 - y, x, z, c)
+    z_peers = [device(y, x, (z + k) % 4, c) for k in (1, 2, 3)]
+    greet([sibling, x_peer, y_peer] + z_peers)
+    copies = Copies(send_sem, recv_sem)
+    state = []
+    for number in range(count):
+        shard, full = shards[number], fulls[number]
+        rows = shard.shape[0]
+        own = pltpu.make_async_copy(shard, full.at[y, x, z, c], local_sem.at[number])
+        own.start()
+        entry = {"own": own, "first": []}
+        if names[number] == "zfirst":
+            for low, high in ((0, rows // 2), (rows // 2, rows)):
+                part = full.at[y, x, z, c, low:high]
+                entry["first"].append([copies.start(shard.at[low:high], part, peer) for peer in z_peers])
+        else:
+            entry["first"].append([copies.start(shard, full.at[y, x, z, c], x_peer)])
+        state.append(entry)
+
+    def second(number):
+        entry, full = state[number], fulls[number]
+        rows = shards[number].shape[0]
+        half = rows // 2
+        entry["own"].wait()
+        for copy in entry["first"][0]:
+            copy.wait_recv()
+        if names[number] == "zfirst":
+            piece = full.at[y, x, :, c, 0:half]
+            entry["a"] = copies.start(piece, piece, x_peer)
+            for copy in entry["first"][1]:
+                copy.wait_recv()
+            piece = full.at[y, x, :, c, half:rows]
+            entry["b"] = copies.start(piece, piece, y_peer)
+        else:
+            piece = full.at[y, :, z, c]
+            entry["a"] = copies.start(piece, piece, y_peer)
+
+    def third(number):
+        entry, full = state[number], fulls[number]
+        rows = shards[number].shape[0]
+        half = rows // 2
+        entry["a"].wait_recv()
+        if names[number] == "zfirst":
+            piece = full.at[y, :, :, c, 0:half]
+            entry["c"] = [copies.start(piece, piece, y_peer)]
+            entry["b"].wait_recv()
+            piece = full.at[:, x, :, c, half:rows]
+            entry["c"].append(copies.start(piece, piece, x_peer))
+        else:
+            piece = full.at[:, :, z, c]
+            entry["c"] = [copies.start(piece, piece, peer) for peer in z_peers]
+
+    def fourth(number):
+        entry, full = state[number], fulls[number]
+        for copy in entry["c"]:
+            copy.wait_recv()
+        piece = full.at[:, :, :, c]
+        entry["d"] = copies.start(piece, piece, sibling)
+
+    stages = (second, third, fourth)
+    for step in range(count + len(stages) - 1):
+        for lag, stage in enumerate(stages):
+            if 0 <= step - lag < count:
+                stage(step - lag)
+    for entry in state:
+        entry["d"].wait_recv()
+    copies.drain()
+
+
+def gather_all(shards, orders):
+    total = sum(11 if order == "zfirst" else 6 for order in orders)
+    return pl.pallas_call(
+        partial(gather_kernel, orders),
+        out_shape=[jax.ShapeDtypeStruct((2, 2, 4, 2) + a.shape, a.dtype) for a in shards],
+        in_specs=[pl.BlockSpec(memory_space=pl.ANY)] * len(shards),
+        out_specs=[pl.BlockSpec(memory_space=pl.ANY)] * len(shards),
+        scratch_shapes=[
+            pltpu.SemaphoreType.DMA((total,)),
+            pltpu.SemaphoreType.DMA((total,)),
+            pltpu.SemaphoreType.DMA((len(shards),)),
+        ],
+        compiler_params=pltpu.CompilerParams(collective_id=1, has_side_effects=True),
+        name="gather_all",
+    )(*shards)
+
+
+def reduce_kernel(orders, *refs):
+    count = len(orders)
+    partials, outs = refs[:count], refs[count : 2 * count]
+    small_ref, small_out = refs[2 * count], refs[2 * count + 1]
+    at = 2 * count + 2
+    own, sib, one, two, three = [refs[at + i * count : at + (i + 1) * count] for i in range(5)]
+    at += 5 * count
+    small_own, small_got, send_sem, recv_sem, local_sem = refs[at:]
+    y, x, z, c = place()
+    sibling, x_peer, y_peer = device(y, x, z, 1 - c), device(y, 1 - x, z, c), device(1 - y, x, z, c)
+    z_peers = [device(y, x, (z + k) % 4, c) for k in (1, 2, 3)]
+    greet([sibling, x_peer, y_peer] + z_peers)
+    copies = Copies(send_sem, recv_sem)
+    state = []
+    for number in range(count):
+        local = pltpu.make_async_copy(
+            partials[number].at[:, :, :, c], own[number], local_sem.at[number]
+        )
+        local.start()
+        state.append(
+            {"local": local, "s": copies.start(partials[number].at[:, :, :, 1 - c], sib[number], sibling)}
+        )
+
+    def add_in(total, extra, where, shards):
+        def body(i, carry):
+            index = where(i)
+            total[index] = total[index] + extra(i)
+            return carry
+
+        lax.fori_loop(0, shards, body, 0)
+
+    def first(number):
+        entry, total, got = state[number], own[number], sib[number]
+        rows = total.shape[3]
+        half = rows // 2
+        entry["local"].wait()
+        entry["s"].wait_recv()
+        add_in(total, lambda i: got[i // 8, i // 4 % 2, i % 4], lambda i: (i // 8, i // 4 % 2, i % 4), 16)
+        if orders[number] == "zlast":
+            entry["a"] = copies.start(
+                total.at[1 - y, :, :, 0:half], one[number].at[0], y_peer
+            )
+            entry["b"] = copies.start(
+                total.at[:, 1 - x, :, half:rows], one[number].at[1], x_peer
+            )
+        else:
+            entry["a"] = [
+                copies.start(total.at[:, :, (z + k) % 4], one[number].at[k - 1], z_peers[k - 1])
+                for k in (1, 2, 3)
+            ]
+
+    def second(number):
+        entry, total, got = state[number], own[number], one[number]
+        rows = total.shape[3]
+        half = rows // 2
+        if orders[number] == "zlast":
+            entry["a"].wait_recv()
+            add_in(
+                total,
+                lambda i: got[0, i // 4, i % 4],
+                lambda i: (y, i // 4, i % 4, slice(0, half)),
+                8,
+            )
+            entry["c"] = copies.start(total.at[y, 1 - x, :, 0:half], two[number].at[0], x_peer)
+            entry["b"].wait_recv()
+            add_in(
+                total,
+                lambda i: got[1, i // 4, i % 4],
+                lambda i: (i // 4, x, i % 4, slice(half, rows)),
+                8,
+            )
+            entry["d"] = copies.start(total.at[1 - y, x, :, half:rows], two[number].at[1], y_peer)
+        else:
+            for copy in entry["a"]:
+                copy.wait_recv()
+            add_in(
+                total,
+                lambda i: got[0, i // 2, i % 2] + got[1, i // 2, i % 2] + got[2, i // 2, i % 2],
+                lambda i: (i // 2, i % 2, z),
+                4,
+            )
+            entry["c"] = copies.start(total.at[1 - y, :, z], two[number], y_peer)
+
+    def third(number):
+        entry, total, got = state[number], own[number], two[number]
+        rows = total.shape[3]
+        half = rows // 2
+        entry["c"].wait_recv()
+        if orders[number] == "zlast":
+            add_in(total, lambda i: got[0, i], lambda i: (y, x, i, slice(0, half)), 4)
+            entry["d"].wait_recv()
+            add_in(total, lambda i: got[1, i], lambda i: (y, x, i, slice(half, rows)), 4)
+            entry["e"] = [
+                copies.start(total.at[y, x, (z + k) % 4], three[number].at[k - 1], z_peers[k - 1])
+                for k in (1, 2, 3)
+            ]
+        else:
+            add_in(total, lambda i: got[i], lambda i: (y, i, z), 2)
+            entry["e"] = [copies.start(total.at[y, 1 - x, z], three[number], x_peer)]
+
+    def fourth(number):
+        entry, total, got, out = state[number], own[number], three[number], outs[number]
+        for copy in entry["e"]:
+            copy.wait_recv()
+        value = total[y, x, z].astype(jnp.float32)
+        if orders[number] == "zlast":
+            for k in range(3):
+                value = value + got[k].astype(jnp.float32)
+        else:
+            value = value + got[...].astype(jnp.float32)
+        out[...] = value
+
+    def small(step):
+        if step == 0:
+            small_own[...] = small_ref[...]
+        elif step < 4:
+            copies_small[-1].wait()
+            small_own[...] = small_own[...] + small_got[step - 1]
+        peer = (sibling, x_peer, y_peer)[step] if step < 3 else None
+        if peer is not None:
+            copy = pltpu.make_async_remote_copy(
+                src_ref=small_own,
+                dst_ref=small_got.at[step],
+                send_sem=send_sem.at[total_copies + step],
+                recv_sem=recv_sem.at[total_copies + step],
+                device_id=peer,
+                device_id_type=MESH,
+            )
+            copy.start()
+            copies_small.append(copy)
+        else:
+            small_got[3 + z] = small_own[...]
+            for k in (1, 2, 3):
+                copy = pltpu.make_async_remote_copy(
+                    src_ref=small_own,
+                    dst_ref=small_got.at[3 + z],
+                    send_sem=send_sem.at[total_copies + 2 + k],
+                    recv_sem=recv_sem.at[total_copies + 2 + k],
+                    device_id=z_peers[k - 1],
+                    device_id_type=MESH,
+                )
+                copy.start()
+                copies_small.append(copy)
+
+    total_copies = copies_of(orders, 9, 6)
+    copies_small = []
+    stages = (first, second, third, fourth)
+    for step in range(count + len(stages) - 1):
+        for lag, stage in enumerate(stages):
+            if 0 <= step - lag < count:
+                stage(step - lag)
+        if step < 4:
+            small(step)
+    for copy in copies_small[3:]:
+        copy.wait()
+    small_out[...] = small_got[3] + small_got[4] + small_got[5] + small_got[6]
+    copies.drain()
+
+
+def copies_of(orders, zlast, zfirst):
+    return sum(zlast if order == "zlast" else zfirst for order in orders)
+
+
+def reduce_all(partials, orders, small):
+    count = len(partials)
+    shapes = [a.shape[4:] for a in partials]
+
+    def scratch(first, other):
+        return [
+            pltpu.VMEM((first(r) if o == "zlast" else other(r)) + (n,), jnp.bfloat16)
+            for o, (r, n) in zip(orders, shapes)
+        ]
+
+    total = copies_of(orders, 9, 6) + 6
+    vmem = pl.BlockSpec(memory_space=pltpu.VMEM)
+    return pl.pallas_call(
+        partial(reduce_wrap, orders),
+        out_shape=[jax.ShapeDtypeStruct(shape, jnp.float32) for shape in shapes]
+        + [jax.ShapeDtypeStruct(small.shape, jnp.float32)],
+        in_specs=[pl.BlockSpec(memory_space=pl.ANY)] * count + [vmem],
+        out_specs=[vmem] * (count + 1),
+        scratch_shapes=scratch(lambda r: (2, 2, 4, r), lambda r: (2, 2, 4, r))
+        + scratch(lambda r: (2, 2, 4, r), lambda r: (2, 2, 4, r))
+        + scratch(lambda r: (2, 2, 4, r // 2), lambda r: (3, 2, 2, r))
+        + scratch(lambda r: (2, 4, r // 2), lambda r: (2, r))
+        + scratch(lambda r: (3, r), lambda r: (r,))
+        + [
+            pltpu.VMEM(small.shape, jnp.float32),
+            pltpu.VMEM((7,) + small.shape, jnp.float32),
+            pltpu.SemaphoreType.DMA((total,)),
+            pltpu.SemaphoreType.DMA((total,)),
+            pltpu.SemaphoreType.DMA((count,)),
+        ],
+        compiler_params=pltpu.CompilerParams(
+            collective_id=2, has_side_effects=True, vmem_limit_bytes=60 * 2**20
+        ),
+        name="reduce_all",
+    )(*partials, small)
+
+
+def reduce_wrap(orders, *refs):
+    count = len(orders)
+    partials, small_ref = refs[:count], refs[count]
+    outs, small_out = refs[count + 1 : 2 * count + 1], refs[2 * count + 1]
+    reduce_kernel(orders, *partials, *outs, small_ref, small_out, *refs[2 * count + 2 :])
+
+
+def plane_peer(h, rel):
+    return h + (rel % 2) * (1 - 2 * (h % 2)) + (rel // 2) * (2 - 4 * (h // 2))
+
+
+def attend_kernel(scaling, live_ref, triple, out, spread, logsum, staged, send_sem, recv_sem, local_sem):
+    h, s = lax.axis_index("head"), lax.axis_index("seq")
+    rows, slot_rows = triple.shape[0], spread.shape[0]
+    wide = spread.shape[1]
+    narrow = staged.shape[1]
+    heads = narrow // DH
+    greet([(plane_peer(h, rel), s) for rel in (1, 2, 3)])
+
+    def into(rel):
+        peer = plane_peer(h, rel)
+        return pltpu.make_async_remote_copy(
+            src_ref=triple.at[:, pl.ds(pl.multiple_of(peer * wide, 128), wide)],
+            dst_ref=spread.at[pl.ds(pl.multiple_of(h * rows, rows), rows), :],
+            send_sem=send_sem.at[rel - 1],
+            recv_sem=recv_sem.at[rel - 1],
+            device_id=(peer, s),
+            device_id_type=MESH,
+        )
+
+    def back(rel):
+        peer = plane_peer(h, rel)
+        return pltpu.make_async_remote_copy(
+            src_ref=staged.at[pl.ds(pl.multiple_of(peer * rows, rows), rows), :],
+            dst_ref=out.at[:, pl.ds(pl.multiple_of(h * narrow, 128), narrow)],
+            send_sem=send_sem.at[2 + rel],
+            recv_sem=recv_sem.at[2 + rel],
+            device_id=(peer, s),
+            device_id_type=MESH,
+        )
+
+    moved = [into(rel) for rel in (3, 1, 2)]
+    for copy in moved:
+        copy.start()
+    own = pltpu.make_async_copy(
+        triple.at[:, pl.ds(pl.multiple_of(h * wide, 128), wide)],
+        spread.at[pl.ds(pl.multiple_of(h * rows, rows), rows), :],
+        local_sem,
+    )
+    own.start()
+    own.wait()
+    for copy in moved:
+        copy.wait()
+    live = live_ref[0]
+    key_live = lax.broadcasted_iota(jnp.int32, (slot_rows, 1), 0) < live
+
+    def block(turn, carry):
+        rel = 3 - turn
+        peer = plane_peer(h, rel)
+        at = pl.ds(pl.multiple_of(peer * rows, rows), rows)
+        for number in range(heads):
+            base = number * 3 * DH
+            queries = spread[at, base : base + DH]
+            keys = spread[:, base + DH : base + 2 * DH]
+            values = spread[:, base + 2 * DH : base + 3 * DH]
+            scores = lax.dot_general(
+                keys, queries, (((1,), (1,)), ((), ())), preferred_element_type=jnp.float32
+            )
+            scores = jnp.where(key_live, scores * (scaling * LOG2E), -1e30)
+            highest = jnp.max(scores, axis=0, keepdims=True)
+            raw = jnp.exp2(scores - highest)
+            totals = jnp.sum(raw, axis=0, keepdims=True)
+            weights = (raw * (1.0 / totals)).astype(jnp.bfloat16)
+            mixed = lax.dot_general(
+                values, weights, (((0,), (0,)), ((), ())), preferred_element_type=jnp.float32
+            )
+            staged[at, number * DH : (number + 1) * DH] = mixed.T.astype(jnp.bfloat16)
+            logsum[number, at] = (highest + jnp.log2(totals))[0]
+
+        @pl.when(rel > 0)
+        def _():
+            back(rel).start()
+
+        return carry
+
+    lax.fori_loop(0, 4, block, 0)
+    own = pltpu.make_async_copy(
+        staged.at[pl.ds(pl.multiple_of(h * rows, rows), rows), :],
+        out.at[:, pl.ds(pl.multiple_of(h * narrow, 128), narrow)],
+        local_sem,
+    )
+    own.start()
+    own.wait()
+    for rel in (3, 2, 1):
+        back(rel).wait()
+
+
+def attend(live, triple, scaling):
+    rows, width = triple.shape
+    slot_rows, wide = rows * 4, width // 4
+    vmem = pl.BlockSpec(memory_space=pltpu.VMEM)
+    return pl.pallas_call(
+        partial(attend_kernel, scaling),
+        out_shape=[
+            jax.ShapeDtypeStruct((rows, width // 3), jnp.bfloat16),
+            jax.ShapeDtypeStruct((slot_rows, wide), jnp.bfloat16),
+            jax.ShapeDtypeStruct((8, slot_rows), jnp.float32),
+        ],
+        in_specs=[pl.BlockSpec(memory_space=pltpu.SMEM), vmem],
+        out_specs=[vmem] * 3,
+        scratch_shapes=[
+            pltpu.VMEM((slot_rows, wide // 3), jnp.bfloat16),
+            pltpu.SemaphoreType.DMA((6,)),
+            pltpu.SemaphoreType.DMA((6,)),
+            pltpu.SemaphoreType.DMA,
+        ],
+        compiler_params=pltpu.CompilerParams(
+            collective_id=3, has_side_effects=True, vmem_limit_bytes=48 * 2**20
+        ),
+        name="attend",
+    )(live, triple)
+
+
+def attend_back_kernel(
+    scaling, live_ref, d_rows, spread, logsum, d_triple, d_out, d_spread, grad_keys, grad_values, send_sem, recv_sem, local_sem
+):
+    h, s = lax.axis_index("head"), lax.axis_index("seq")
+    rows, slot_rows = d_rows.shape[0], spread.shape[0]
+    wide = spread.shape[1]
+    narrow = d_out.shape[1]
+    heads = narrow // DH
+    greet([(plane_peer(h, rel), s) for rel in (1, 2, 3)])
+
+    def into(rel):
+        peer = plane_peer(h, rel)
+        return pltpu.make_async_remote_copy(
+            src_ref=d_rows.at[:, pl.ds(pl.multiple_of(peer * narrow, 128), narrow)],
+            dst_ref=d_out.at[pl.ds(pl.multiple_of(h * rows, rows), rows), :],
+            send_sem=send_sem.at[rel - 1],
+            recv_sem=recv_sem.at[rel - 1],
+            device_id=(peer, s),
+            device_id_type=MESH,
+        )
+
+    def back(rel):
+        peer = plane_peer(h, rel)
+        return pltpu.make_async_remote_copy(
+            src_ref=d_spread.at[pl.ds(pl.multiple_of(peer * rows, rows), rows), :],
+            dst_ref=d_triple.at[:, pl.ds(pl.multiple_of(h * wide, 128), wide)],
+            send_sem=send_sem.at[2 + rel],
+            recv_sem=recv_sem.at[2 + rel],
+            device_id=(peer, s),
+            device_id_type=MESH,
+        )
+
+    moved = [into(rel) for rel in (3, 1, 2)]
+    for copy in moved:
+        copy.start()
+    own = pltpu.make_async_copy(
+        d_rows.at[:, pl.ds(pl.multiple_of(h * narrow, 128), narrow)],
+        d_out.at[pl.ds(pl.multiple_of(h * rows, rows), rows), :],
+        local_sem,
+    )
+    own.start()
+    own.wait()
+    for copy in moved:
+        copy.wait()
+    live = live_ref[0]
+    key_live = lax.broadcasted_iota(jnp.int32, (slot_rows, 1), 0) < live
+
+    for number in range(heads):
+        base = number * 3 * DH
+        grad_keys[...] = jnp.zeros_like(grad_keys)
+        grad_values[...] = jnp.zeros_like(grad_values)
+
+        def block(turn, carry, number=number, base=base):
+            at = pl.ds(pl.multiple_of(turn * rows, rows), rows)
+            queries = spread[at, base : base + DH]
+            keys = spread[:, base + DH : base + 2 * DH]
+            values = spread[:, base + 2 * DH : base + 3 * DH]
+            grads = d_out[at, number * DH : (number + 1) * DH]
+            scores = lax.dot_general(
+                keys, queries, (((1,), (1,)), ((), ())), preferred_element_type=jnp.float32
+            )
+            powers = scores * (scaling * LOG2E) - logsum[number, at][None, :]
+            weights = jnp.where(key_live, jnp.exp2(powers), 0.0)
+            grad_values[...] += jnp.dot(
+                weights.astype(jnp.bfloat16), grads, preferred_element_type=jnp.float32
+            )
+            grad_weights = lax.dot_general(
+                values, grads, (((1,), (1,)), ((), ())), preferred_element_type=jnp.float32
+            )
+            deltas = jnp.sum(grad_weights * weights, axis=0, keepdims=True)
+            grad_scores = (weights * (grad_weights - deltas)).astype(jnp.bfloat16)
+            grad_keys[...] += jnp.dot(grad_scores, queries, preferred_element_type=jnp.float32)
+            grad_queries = lax.dot_general(
+                keys, grad_scores, (((0,), (0,)), ((), ())), preferred_element_type=jnp.float32
+            )
+            d_spread[at, base : base + DH] = (grad_queries.T * scaling).astype(jnp.bfloat16)
+            return carry
+
+        lax.fori_loop(0, 4, block, 0)
+        d_spread[:, base + DH : base + 2 * DH] = (grad_keys[...] * scaling).astype(jnp.bfloat16)
+        d_spread[:, base + 2 * DH : base + 3 * DH] = grad_values[...].astype(jnp.bfloat16)
+    returned = [back(rel) for rel in (3, 1, 2)]
+    for copy in returned:
+        copy.start()
+    own = pltpu.make_async_copy(
+        d_spread.at[pl.ds(pl.multiple_of(h * rows, rows), rows), :],
+        d_triple.at[:, pl.ds(pl.multiple_of(h * wide, 128), wide)],
+        local_sem,
+    )
+    own.start()
+    own.wait()
+    for copy in returned:
+        copy.wait()
+
+
+def attend_backward(live, d_rows, spread, logsum, scaling):
+    rows, features = d_rows.shape
+    slot_rows, wide = spread.shape
+    vmem = pl.BlockSpec(memory_space=pltpu.VMEM)
+    return pl.pallas_call(
+        partial(attend_back_kernel, scaling),
+        out_shape=jax.ShapeDtypeStruct((rows, 3 * features), jnp.bfloat16),
+        in_specs=[pl.BlockSpec(memory_space=pltpu.SMEM), vmem, vmem, vmem],
+        out_specs=vmem,
+        scratch_shapes=[
+            pltpu.VMEM((slot_rows, wide // 3), jnp.bfloat16),
+            pltpu.VMEM((slot_rows, wide), jnp.bfloat16),
+            pltpu.VMEM((slot_rows, DH), jnp.float32),
+            pltpu.VMEM((slot_rows, DH), jnp.float32),
+            pltpu.SemaphoreType.DMA((6,)),
+            pltpu.SemaphoreType.DMA((6,)),
+            pltpu.SemaphoreType.DMA,
+        ],
+        compiler_params=pltpu.CompilerParams(
+            collective_id=4, has_side_effects=True, vmem_limit_bytes=48 * 2**20
+        ),
+        name="attend_back",
+    )(live, d_rows, spread, logsum)
+
+
+def hop(value, pairs):
+    return lax.ppermute(value, "head", pairs)
+
+
+def matmul(left, right):
+    return jnp.dot(left, right, preferred_element_type=jnp.float32)
+
+
+def matmul_nt(left, right):
+    return lax.dot_general(left, right, (((1,), (1,)), ((), ())), preferred_element_type=jnp.float32)
+
+
+def matmul_tn(left, right):
+    return lax.dot_general(left, right, (((0,), (0,)), ((), ())), preferred_element_type=jnp.float32)
+
+
+def body_planned(
+    tokens,
+    patch_counts,
+    w_qkv,
+    w_out,
+    w_up,
+    w_down,
+    w_patch,
+    w_class,
+    norm_gains,
+    mask_norm,
+    grad_masks,
+):
+    gain_tile = jnp.pad(norm_gains, ((0, 14), (0, 96)))
+    orders = ("zfirst", "zfirst", "xfirst", "zfirst", "zfirst", "zfirst", "xfirst")
+    shards = (gain_tile, w_qkv, w_out, w_up, w_down, w_patch, w_class)
+    fulls = gather_all(shards, orders)
+    full_gains = fulls[0].reshape(32, 16, 128)[:, :2, :32].transpose(1, 0, 2).reshape(2, 1024)
+    full_qkv, full_out, full_up, full_down, full_patch, full_class = [
+        a.reshape(-1, a.shape[-1]) for a in fulls[1:]
+    ]
+    gain_one = full_gains[0].astype(jnp.float32)
+    gain_two = full_gains[1].astype(jnp.float32)
+    tokens, grad_masks = tokens[0], grad_masks[0]
+    row_count = tokens.shape[0]
+    h = lax.axis_index("head")
+    position = h * row_count + jnp.arange(row_count, dtype=jnp.int32)
+    live = CLS + patch_counts
+    patch_rows = ((position >= CLS) & (position < live[0])).astype(jnp.float32)[:, None]
+    root_flag = (h == 0).astype(jnp.float32)
+    scaling = DH ** (-0.5)
+
+    normal_one, inverse_one = standardize(tokens)
+    normed_one = (normal_one * gain_one).astype(jnp.bfloat16)
+    triple = matmul(normed_one, full_qkv).astype(jnp.bfloat16)
+    attended, spread, logsum = attend(live, triple, scaling)
+    second = tokens + matmul(attended, full_out)
+    normal_two, inverse_two = standardize(second)
+    normed_two = (normal_two * gain_two).astype(jnp.bfloat16)
+    hidden = matmul(normed_two, full_up)
+    gelu_exact = partial(jax.nn.gelu, approximate=False)
+    active = gelu_exact(hidden).astype(jnp.bfloat16)
+    residual = second + matmul(active, full_down)
+    rounded = residual.astype(jnp.bfloat16)
+    class_rows = rounded[:CLS]
+    class_proj = matmul(class_rows, full_class)
+    class_unit = (class_proj * unit_scale(class_proj)).astype(jnp.bfloat16)
+    arrived = [hop(class_unit, [(0, rel)]) for rel in (1, 2, 3)]
+    patch_proj = matmul(rounded, full_patch)
+    patch_unit = (patch_proj * unit_scale(patch_proj)).astype(jnp.bfloat16)
+    classes = jnp.where(h == 0, class_unit, arrived[0] + arrived[1] + arrived[2])
+    products = matmul_nt(patch_unit, classes)
+    normal_mask, inverse_mask = standardize(products)
+    class_masks = (normal_mask * mask_norm[0] + mask_norm[1]) * patch_rows
+    upstream = grad_masks * patch_rows
+    mask_sums = jnp.stack([jnp.sum(upstream * normal_mask, axis=0), jnp.sum(upstream, axis=0)])
+    d_products = standard_back(normal_mask, inverse_mask, upstream * mask_norm[0]).astype(jnp.bfloat16)
+    class_part = matmul_tn(d_products, patch_unit)
+    class_sent = class_part.astype(jnp.bfloat16)
+    parts = [hop(class_sent, [(rel, 0)]) for rel in (1, 2, 3)]
+    d_patch_unit = matmul(d_products, classes)
+    d_patch_proj = unit_back(patch_proj, d_patch_unit).astype(jnp.bfloat16)
+    d_class_unit = class_part + (
+        parts[0].astype(jnp.float32) + parts[1].astype(jnp.float32) + parts[2].astype(jnp.float32)
+    )
+    d_class_proj = (unit_back(class_proj, d_class_unit) * root_flag).astype(jnp.bfloat16)
+    grad_patch = matmul_tn(rounded, d_patch_proj).astype(jnp.bfloat16)
+    grad_class = matmul_tn(class_rows, d_class_proj).astype(jnp.bfloat16)
+    d_residual = matmul_nt(d_patch_proj, full_patch)
+    d_residual = d_residual.at[:CLS].add(matmul_nt(d_class_proj, full_class))
+    d_branch = d_residual.astype(jnp.bfloat16)
+    grad_down = matmul_tn(active, d_branch).astype(jnp.bfloat16)
+    d_active = matmul_nt(d_branch, full_down)
+    d_hidden = jax.vjp(gelu_exact, hidden)[1](d_active)[0].astype(jnp.bfloat16)
+    grad_up = matmul_tn(normed_two, d_hidden).astype(jnp.bfloat16)
+    d_normed_two = matmul_nt(d_hidden, full_up)
+    d_second = d_residual + standard_back(normal_two, inverse_two, d_normed_two * gain_two)
+    grad_gain_two = jnp.sum(d_normed_two * normal_two, axis=0)
+    d_mix = d_second.astype(jnp.bfloat16)
+    grad_out = matmul_tn(attended, d_mix).astype(jnp.bfloat16)
+    d_attended = matmul_nt(d_mix, full_out).astype(jnp.bfloat16)
+    d_triple = attend_backward(live, d_attended, spread, logsum, scaling)
+    grad_qkv = matmul_tn(normed_one, d_triple).astype(jnp.bfloat16)
+    d_normed_one = matmul_nt(d_triple, full_qkv)
+    grad_inputs = d_second + standard_back(normal_one, inverse_one, d_normed_one * gain_one)
+    grad_gain_one = jnp.sum(d_normed_one * normal_one, axis=0)
+    small = jnp.concatenate(
+        [jnp.stack([grad_gain_one, grad_gain_two]), jnp.pad(mask_sums, ((0, 0), (0, 1024 - CLS)))]
+    )
+    partials = [
+        a.reshape(2, 2, 4, 2, a.shape[0] // 32, a.shape[1])
+        for a in (grad_qkv, grad_out, grad_up, grad_down, grad_patch, grad_class)
+    ]
+    reduced = reduce_all(
+        partials, ("zlast", "zfirst", "zlast", "zlast", "zlast", "zfirst"), small
+    )
+    sums = reduced[6]
+    place_at = (h * 8 + lax.axis_index("seq")) * 32
+    grad_gains = lax.dynamic_slice(sums, (0, place_at), (2, 32))
+    return (
+        class_masks[None],
+        grad_inputs[None],
+        *reduced[:6],
+        grad_gains,
+        sums[2:4, :CLS],
+    )
+
+
 def solution(mesh):
+    planned = dict(mesh.shape) == {"head": 4, "seq": 8}
     return jax.shard_map(
-        body,
+        body_planned if planned else body_general,
         mesh=mesh,
         in_specs=(
             P("seq", "head", None),

time: 1830 us -> 565 us (0.31)
  waiting for transfers between devices: 1360 us -> 14 us
  Pallas kernels: 0 us -> 431 us
  matrix products: 182 us -> 76.9 us
  blocking collectives: 105 us -> 0 us
  local copies, waits for them, and re-layouts: 84.2 us -> 15.2 us
  other arithmetic: 63.8 us -> 8.98 us
    reduce_scatter x6 -> x0, waiting for transfers between devices: 961 us -> none  [the longest x1 189 us: body(): lax.psum_scatter(grad_up, ('head', 'seq'), scatter_dimension=0, tiled=True)]
    pallas_call x0 -> x4, Pallas kernels: none -> 431 us  [the longest x1 179 us: reduce_all(): pl.pallas_call(partial(reduce_wrap, orders), out_shape=[jax.ShapeDtypeStr...]
    all_gather x6 -> x0, waiting for transfers between devices: 223 us -> none  [the longest x1 63.2 us: body(): lax.all_gather(w_down, ('head', 'seq'), axis=0, tiled=True)]
    dot_general x77 -> x21, matrix products: 182 us -> 76.9 us  [the longest x7 28.7 us: matmul(): return jnp.dot(left, right, preferred_element_type=jnp.float32)]
    psum x2 -> x0, waiting for transfers between devices: 83.8 us -> none  [the longest x1 43.2 us: spread_2(): return lax.psum(kept, axis)]
    unnamed x16 -> x0, waiting for transfers between devices: 51.3 us -> none
    all_gather x1 -> x0, blocking collectives: 43.2 us -> none  [body(): lax.all_gather(gains_rows, ('head', 'seq'), axis=0, tiled=True)]
    psum x1 -> x0, blocking collectives: 39.4 us -> none  [body(): lax.psum(jnp.stack([jnp.sum(upstream * normal_mask, axis=(0, 1)), jnp.sum...]
  transfers between devices with their start and end apart: 18 -> 6, of which waited for: 17 -> 3; matrix products, arithmetic and copies ran while one was open for 8% -> 1% of each run, Pallas kernels for 0% -> 0%
where the time goes in v1:
time: 565 us; the launch traced here: 561 us
  Pallas kernels  431 us (76%)
  matrix products  76.9 us (14%)
  local copies, waits for them, and re-layouts  15.2 us (3%)
  waiting for transfers between devices  14 us (2%)
  starting transfers between devices  12.7 us (2%)
  other arithmetic  8.98 us (2%)
    pallas_call x1, Pallas kernels, reduce_all(): pl.pallas_call(partial(reduce_wrap, orders), out_shape=[jax.ShapeDtypeStr...  179 us
    pallas_call x1, Pallas kernels, gather_all(): pl.pallas_call(partial(gather_kernel, orders), out_shape=[jax.ShapeDtypeS...  167 us
    pallas_call x1, Pallas kernels, attend_backward(): pl.pallas_call(partial(attend_back_kernel, scaling), out_shape=jax.ShapeD...  49 us
    pallas_call x1, Pallas kernels, attend(): pl.pallas_call(partial(attend_kernel, scaling), out_shape=[jax.ShapeDtype...  36.3 us
    dot_general x7, matrix products, matmul(): return jnp.dot(left, right, preferred_element_type=jnp.float32)  28.7 us
    dot_general x7, matrix products, matmul_nt(): lax.dot_general(left, right, (((1,), (1,)), ((), ())), preferred_element_...  25.6 us
    dot_general x7, matrix products, matmul_tn(): lax.dot_general(left, right, (((0,), (0,)), ((), ())), preferred_element_...  22.6 us
    ppermute x6, waiting for transfers between devices, hop(): return lax.ppermute(value, 'head', pairs)  14 us
  transfers between devices with their start and end apart: 6, of which 3 were waited for; matrix products, arithmetic and copies ran while one was open for 1% of the time, Pallas kernels for 0%

profile of v1, /device:TPU:0, one launch (start us, length us, event | category | flops | bytes accessed | tf_op | source)
XLA Modules:
  0.0 561.1 jit_solution(5315375442766243932)
XLA Ops:
  2.5 166.9 %gather_all.1 = (bf16[2,2,4,2,16,128]{5,4,3,2,1,0:T(8,128)(2,1)}, bf16[2,2,4,2,32,3072]{5,4,3,2,1,0:T(8,128)(2,1)}, bf16[2,2,4,2,32,1024]{5,4,3,2,1,0:T(8,128)(2...) custom-call(bf16[16,128]{1,0:T(8,128)(2,1)} %pad.10.refs_0_, ...), custom_call_target="tpu_custom_call" | custom-call | tf_op jit(solution)/shard_map/gather_all/pallas_call | solution.py:417
  170.5 1.4 reduce_sum.188
  171.9 1.5 multiply_reduce_fusion.7
  173.4 5.1 convolution_convert_fusion.3.triple
  178.6 36.3 %attend.1 = (bf16[256,1024]{1,0:T(8,128)(2,1)S(1)}, bf16[1024,768]{1,0:T(8,128)(2,1)S(1)}, f32[8,1024]{1,0:T(8,128)S(1)}) custom-call(s32[1]{0:T(128)} %add.109.live_ref, bf16[256,3072]{1,0:T(8,128)(2,1)S(1)} %convolution_convert_fusion.3.triple), custom_call_target="tpu_custom_call" | custom-call | tf_op jit(solution)/shard_map/attend/pallas_call | solution.py:733
  216.0 15.9 %multiply_convert_fusion = (bf16[256,4096]{1,0:T(8,128)(2,1)S(1)}, f32[256,4096]{1,0:T(8,128)}, f32[256,4096]{1,0:T(8,128)}) fusion(bf16[1024,4096]{1,0:T(8,128)(2,1)S(1)} %bitcast.110, f32[256,1024]{1,0:T(8,128)S(1)} %get-tuple-element.85, f32[1024]{0:T(1024)S(1)} %reshape.221, f32[256]{0:T(256)S(1)} %add_rsqrt_fusion.3, f32[256]{0:T(256)S(1)} %broadcast_multiply_fusion.7), kind=kOutput, calls=%fused_computation.6 | convolution fusion | flops 2216689664 | bytes 19929088 | tf_op jit(solution)/shard_map/dot_general | solution.py:880
  232.0 2.4 fusion.6
  236.7 4.4 collective-permute-start.2
  241.0 2.0 collective-permute-start
  243.0 2.0 collective-permute-start.1
  245.1 3.4 multiply_reduce_fusion.5
  248.6 5.0 collective-permute-done
  253.5 1.5 add_select_fusion
  255.0 1.7 fusion.35
  260.5 1.7 collective-permute-start.3
  264.0 2.1 convolution_convert_fusion.4
  266.1 2.5 collective-permute-done.5
  268.6 6.6 %collective-permute-done.4 = bf16[150,1024]{1,0:T(8,128)(2,1)S(1)} collective-permute-done((bf16[150,1024]{1,0:T(8,128)(2,1)S(1)}, bf16[150,1024]{1,0:T(8,128)(2,1)S(1)}, u32[]{:S(2)}, u32[]{:S(2)}) %collective-permute-start.4) | collective-permute-done | bytes 307232 | tf_op jit(solution)/shard_map/ppermute | solution.py:876
  275.7 1.7 convolution_add_fusion.2
  277.4 3.1 scatter-add.4
  280.5 9.7 %add_convert_fusion = bf16[256,4096]{1,0:T(8,128)(2,1)S(1)} fusion(f32[256,4096]{1,0:T(8,128)} %get-tuple-element.79, f32[256,4096]{1,0:T(8,128)} %get-tuple-element.86, bf16[4096,1024]{1,0:T(8,128)(2,1)} %bitcast.111, f32[256,1024]{1,0:T(8,128)} %scatter-add.4), kind=kOutput, calls=%fused_computation.5 | convolution fusion | flops 2162425856 | bytes 19922944 | tf_op jit(solution)/shard_map/dot_general | solution.py:884
  290.2 6.1 %multiply_reduce_fusion = (f32[1024]{0:T(1024)S(1)}, f32[256]{0:T(256)S(1)}, f32[256]{0:T(256)S(1)}, f32[256,1024]{1,0:T(8,128)S(1)}) fusion(f32[256,1024]{1,0:T(8,128)S(1)} %copy-done.3, f32[256]{0:T(256)S(1)} %add_rsqrt_fusion.3, f32[256]{0:T(256)S(1)} %broadcast_multiply_fusion.7, f32[1024]{0:T(1024)S(1)} %reshape.221, ...), kind=kOutput, calls=%fused_computation.30 | convolution fusion | flops 2149579264 | bytes 12595200 | tf_op jit(solution)/shard_map/dot_general | solution.py:884
  298.7 49.0 %attend_back.1 = bf16[256,3072]{1,0:T(8,128)(2,1)S(1)} custom-call(s32[1]{0:T(128)} %add.109.live_ref, bf16[256,1024]{1,0:T(8,128)(2,1)S(1)} %convolution_convert_fusion.7.d_rows, bf16[1024,768]{1,0:T(8,128)(2,1)S(1)} %get-tuple-element.47.spread, f32[8,1024]{1,0:T(8,128)S(1)} %get-tuple-element.48.logsum), custom_call_target="tpu_custom_call" | custom-call | tf_op jit(solution)/shard_map/attend_back/pallas_call | solution.py:854
  347.7 4.9 multiply_reduce_fusion.1
  352.6 4.6 convolution_convert_fusion.2
  357.2 2.1 convolution_convert_fusion.5
  359.3 5.7 %convolution_convert_fusion.1 = bf16[1024,4096]{1,0:T(8,128)(2,1)} fusion(bf16[256,4096]{1,0:T(8,128)(2,1)S(1)} %add_convert_fusion, f32[256,1024]{1,0:T(8,128)S(1)} %copy-done.3, f32[1024]{0:T(1024)S(1)} %reshape.221, f32[256]{0:T(256)S(1)} %add_rsqrt_fusion.3, f32[256]{0:T(256)S(1)} %broadcast_multiply_fusion.7), kind=kOutput, calls=%fused_computation.1 | convolution fusion | flops 2152726528 | bytes 11540480 | tf_op jit(solution)/shard_map/dot_general | solution.py:888
  365.0 5.6 convolution_convert_fusion
  370.6 2.2 convolution_convert_fusion.6
  373.4 179.1 %reduce_all.1 = (f32[32,3072]{1,0:T(8,128)}, f32[32,1024]{1,0:T(8,128)}, f32[32,4096]{1,0:T(8,128)}, f32[128,1024]{1,0:T(8,128)}, f32[32,1024]{1,0:T(8,128)}, /*index=5*/f32[32,1024]{1,0:T(8,128)}, f32[4,1024]{1,0:T(4,128)}) custom-call(bf16[2,2,4,2,32,3072]{5,4,3,2,1,0:T(8,128)(2,1)} %bitcast.89, bf16[2,2,4,2,32,1024]{5,4,3,2,1,0:T(8,128)(2,1)} %bitcast.90, ...), custom_call_target="tpu_custom_call" | custom-call | tf_op jit(solution)/shard_map/reduce_all/pallas_call | solution.py:607
  552.6 1.4 slice.50
  555.3 1.3 add_bitcast_fusion
  (116 shorter events, 20.4 us)
Async XLA Ops:
  173.4 42.5 %slice-start = ((s8[8388608]{0:T(1024)(128)(4,1)}), s8[4194304]{0:T(1024)(128)(4,1)S(1)}, s32[]{:S(2)}) async-start(s8[8388608]{0:T(1024)(128)(4,1)} %bitcast.108), calls=%async_computation | async-start | bytes 8388608
  173.4 41.4 %copy-start = (f32[1,256,1024]{2,1,0:T(8,128)S(1)}, f32[1,256,1024]{2,1,0:T(8,128)}, u32[]{:S(2)}) copy-start(f32[1,256,1024]{2,1,0:T(8,128)} %param.13) | copy-start | bytes 3145732
  173.4 41.4 %copy-start.10 = (bf16[2,2,4,2,32,1024]{5,4,3,2,1,0:T(8,128)(2,1)S(1)}, bf16[2,2,4,2,32,1024]{5,4,3,2,1,0:T(8,128)(2,1)}, u32[]{:S(2)}) copy-start(bf16[2,2,4,2,32,1024]{5,4,3,2,1,0:T(8,128)(2,1)} %get-tuple-element.42) | copy-start | bytes 6291460
  173.4 42.5 %slice-start.1 = ((s8[8388608]{0:T(1024)(128)(4,1)}), s8[4194304]{0:T(1024)(128)(4,1)S(1)}, s32[]{:S(2)}) async-start(s8[8388608]{0:T(1024)(128)(4,1)} %bitcast.108), calls=%async_computation.1 | async-start | bytes 8388608
  214.9 17.1 %slice-start.2 = ((s8[8388608]{0:T(1024)(128)(4,1)}), s8[4194304]{0:T(1024)(128)(4,1)S(1)}, s32[]{:S(2)}) async-start(s8[8388608]{0:T(1024)(128)(4,1)} %bitcast.112), calls=%async_computation.2 | async-start | bytes 8388608
  215.7 16.3 %copy-start.2 = (f32[256,1024]{1,0:T(8,128)}, f32[256,1024]{1,0:T(8,128)S(1)}, u32[]{:S(2)}) copy-start(f32[256,1024]{1,0:T(8,128)S(1)} %get-tuple-element.85) | copy-start | bytes 3145732
  216.0 16.0 %slice-start.3 = ((s8[8388608]{0:T(1024)(128)(4,1)}), s8[4194304]{0:T(1024)(128)(4,1)S(1)}, s32[]{:S(2)}) async-start(s8[8388608]{0:T(1024)(128)(4,1)} %bitcast.112), calls=%async_computation.3 | async-start | bytes 8388608
  234.4 14.2 %copy-start.27 = (f32[2,150]{1,0:T(2,128)S(1)}, f32[2,150]{1,0:T(2,128)}, u32[]{:S(2)}) copy-start(f32[2,150]{1,0:T(2,128)} %param.22) | copy-start | bytes 3604
  235.0 21.8 %copy-start.20 = (f32[1,256,150]{1,0,2:T(1,128)S(1)}, f32[1,256,150]{1,0,2:T(1,128)}, u32[]{:S(2)}) copy-start(f32[1,256,150]{1,0,2:T(1,128)} %param.23) | copy-start | bytes 460804
  236.7 11.9 %collective-permute-start.2 = (bf16[150,1024]{1,0:T(8,128)(2,1)}, bf16[150,1024]{1,0:T(8,128)(2,1)}, u32[]{:S(2)}, u32[]{:S(2)}) collective-permute-start(bf16[150,1024]{1,0:T(8,128)(2,1)} %multiply_convert_fusion.7), channel_id=1, source_target_pairs={{0,24},{1,25},{2,26},{3,27},{4,28},{5,29},{6,30},{7,31}} | collective-permute-start | bytes 921608 | tf_op jit(solution)/shard_map/ppermute | solution.py:876
  241.0 12.5 %collective-permute-start = (bf16[150,1024]{1,0:T(8,128)(2,1)}, bf16[150,1024]{1,0:T(8,128)(2,1)}, u32[]{:S(2)}, u32[]{:S(2)}) collective-permute-start(bf16[150,1024]{1,0:T(8,128)(2,1)} %multiply_convert_fusion.7), channel_id=1, source_target_pairs={{0,8},{1,9},{2,10},{3,11},{4,12},{5,13},{6,14},{7,15}} | collective-permute-start | bytes 921608 | tf_op jit(solution)/shard_map/ppermute | solution.py:876
  243.0 10.5 %collective-permute-start.1 = (bf16[150,1024]{1,0:T(8,128)(2,1)}, bf16[150,1024]{1,0:T(8,128)(2,1)}, u32[]{:S(2)}, u32[]{:S(2)}) collective-permute-start(bf16[150,1024]{1,0:T(8,128)(2,1)} %multiply_convert_fusion.7), channel_id=1, source_target_pairs={{0,16},{1,17},{2,18},{3,19},{4,20},{5,21},{6,22},{7,23}} | collective-permute-start | bytes 921608 | tf_op jit(solution)/shard_map/ppermute | solution.py:876
  248.5 8.6 %copy-start.1 = (f32[256,1024]{1,0:T(8,128)S(1)}, f32[256,1024]{1,0:T(8,128)}, u32[]{:S(2)}) copy-start(f32[256,1024]{1,0:T(8,128)} %get-tuple-element.90) | copy-start | bytes 3145732
  256.7 5.7 %copy-start.14 = (bf16[2,2,4,2,32,1024]{5,4,3,2,1,0:T(8,128)(2,1)S(1)}, bf16[2,2,4,2,32,1024]{5,4,3,2,1,0:T(8,128)(2,1)}, u32[]{:S(2)}) copy-start(bf16[2,2,4,2,32,1024]{5,4,3,2,1,0:T(8,128)(2,1)} %get-tuple-element.45) | copy-start | bytes 6291460
  257.5 6.5 %copy-start.16 = (bf16[256,1024]{1,0:T(8,128)(2,1)S(1)}, bf16[256,1024]{1,0:T(8,128)(2,1)}, u32[]{:S(2)}) copy-start(bf16[256,1024]{1,0:T(8,128)(2,1)} %copy-done.15) | copy-start | bytes 1572868
  257.9 10.7 %collective-permute-start.5 = (bf16[150,1024]{1,0:T(8,128)(2,1)S(1)}, bf16[150,1024]{1,0:T(8,128)(2,1)S(1)}, u32[]{:S(2)}, u32[]{:S(2)}) collective-permute-start(bf16[150,1024]{1,0:T(8,128)(2,1)S(1)} %get-tuple-element.95), channel_id=1, source_target_pairs={{24,0},{25,1},{26,2},{27,3},{28,4},{29,5},{30,6},{31,7}} | collective-permute-start | bytes 921608 | tf_op jit(solution)/shard_map/ppermute | solution.py:876
  259.2 16.0 %collective-permute-start.4 = (bf16[150,1024]{1,0:T(8,128)(2,1)S(1)}, bf16[150,1024]{1,0:T(8,128)(2,1)S(1)}, u32[]{:S(2)}, u32[]{:S(2)}) collective-permute-start(bf16[150,1024]{1,0:T(8,128)(2,1)S(1)} %get-tuple-element.95), channel_id=1, source_target_pairs={{16,0},{17,1},{18,2},{19,3},{20,4},{21,5},{22,6},{23,7}} | collective-permute-start | bytes 921608 | tf_op jit(solution)/shard_map/ppermute | solution.py:876
  260.5 14.7 %collective-permute-start.3 = (bf16[150,1024]{1,0:T(8,128)(2,1)S(1)}, bf16[150,1024]{1,0:T(8,128)(2,1)S(1)}, u32[]{:S(2)}, u32[]{:S(2)}) collective-permute-start(bf16[150,1024]{1,0:T(8,128)(2,1)S(1)} %get-tuple-element.95), channel_id=1, source_target_pairs={{8,0},{9,1},{10,2},{11,3},{12,4},{13,5},{14,6},{15,7}} | collective-permute-start | bytes 921608 | tf_op jit(solution)/shard_map/ppermute | solution.py:876
  262.4 12.7 %copy-start.7 = (f32[150,1024]{1,0:T(8,128)S(1)}, f32[150,1024]{1,0:T(8,128)}, u32[]{:S(2)}) copy-start(f32[150,1024]{1,0:T(8,128)} %copy-done.6) | copy-start | bytes 1843204
  263.2 12.5 %copy-start.8 = (f32[256,1024]{1,0:T(8,128)}, f32[256,1024]{1,0:T(8,128)S(1)}, u32[]{:S(2)}) copy-start(f32[256,1024]{1,0:T(8,128)S(1)} %fusion.37) | copy-start | bytes 3145732
  263.2 12.5 %copy-start.13 = (bf16[2,2,4,2,32,1024]{5,4,3,2,1,0:T(8,128)(2,1)S(1)}, bf16[2,2,4,2,32,1024]{5,4,3,2,1,0:T(8,128)(2,1)}, u32[]{:S(2)}) copy-start(bf16[2,2,4,2,32,1024]{5,4,3,2,1,0:T(8,128)(2,1)} %get-tuple-element.46) | copy-start | bytes 6291460
  280.5 9.7 %copy-start.3 = (f32[256,1024]{1,0:T(8,128)S(1)}, f32[256,1024]{1,0:T(8,128)}, u32[]{:S(2)}) copy-start(f32[256,1024]{1,0:T(8,128)} %copy-done.2) | copy-start | bytes 3145732
  290.2 6.2 %copy-start.9 = (f32[256,1024]{1,0:T(8,128)S(1)}, f32[256,1024]{1,0:T(8,128)}, u32[]{:S(2)}) copy-start(f32[256,1024]{1,0:T(8,128)} %scatter-add.4) | copy-start | bytes 3145732
  297.9 59.3 %copy-start.4 = (f32[256,1024]{1,0:T(8,128)}, f32[256,1024]{1,0:T(8,128)S(1)}, u32[]{:S(2)}) copy-start(f32[256,1024]{1,0:T(8,128)S(1)} %multiply_add_fusion) | copy-start | bytes 3145732
  359.3 5.7 %copy-start.19 = (bf16[256,4096]{1,0:T(8,128)(2,1)S(1)}, bf16[256,4096]{1,0:T(8,128)(2,1)}, u32[]{:S(2)}) copy-start(bf16[256,4096]{1,0:T(8,128)(2,1)} %copy-done.18) | copy-start | bytes 6291460
  365.0 5.6 copy-start.17
  373.4 181.9 %copy-start.5 = (f32[256,1024]{1,0:T(8,128)S(1)}, f32[256,1024]{1,0:T(8,128)}, u32[]{:S(2)}) copy-start(f32[256,1024]{1,0:T(8,128)} %copy-done.4) | copy-start | bytes 3145732
  552.6 4.8 copy-start.26
  552.6 5.5 copy-start.22
  552.6 6.3 %copy-start.21 = (f32[128,1024]{1,0:T(8,128)S(1)}, f32[128,1024]{1,0:T(8,128)}, u32[]{:S(2)}) copy-start(f32[128,1024]{1,0:T(8,128)} %get-tuple-element.116) | copy-start | bytes 1572868
  552.6 7.0 %copy-start.25 = (f32[32,1024]{1,0:T(8,128)S(1)}, f32[32,1024]{1,0:T(8,128)}, u32[]{:S(2)}) copy-start(f32[32,1024]{1,0:T(8,128)} %get-tuple-element.117) | copy-start | bytes 393220
  552.6 7.7 %copy-start.24 = (f32[32,1024]{1,0:T(8,128)S(1)}, f32[32,1024]{1,0:T(8,128)}, u32[]{:S(2)}) copy-start(f32[32,1024]{1,0:T(8,128)} %get-tuple-element.118) | copy-start | bytes 393220
  (6 other events, 13.7 us)

commit v2 on v0

--- a/solution.py
+++ b/solution.py
@@ -3,6 +3,8 @@
 import jax
 import jax.numpy as jnp
 from jax import lax
+from jax.experimental import pallas as pl
+from jax.experimental.pallas import tpu as pltpu
 from jax.sharding import PartitionSpec as P
 
 HEADS = 16
@@ -100,7 +102,7 @@
     return (grad_queries.reshape(-1, head_width), grad_keys, grad_values)
 
 
-def body(
+def body_general(
     tokens,
     patch_counts,
     w_qkv,
@@ -292,9 +294,856 @@
     )
 
 
+MESH = pl.DeviceIdType.MESH
+LOG2E = 1.4426950408889634
+SLOTS = 16
+
+
+def device(y, x, z, c):
+    return (y * 2 + x, z * 2 + c)
+
+
+class Links:
+    def __init__(self, send_sem, recv_sem):
+        head, seq = lax.axis_index("head"), lax.axis_index("seq")
+        self.y, self.x, self.z, self.c = head // 2, head % 2, seq // 2, seq % 2
+        y, x, z, c = self.y, self.x, self.z, self.c
+        self.sibling = device(y, x, z, 1 - c)
+        self.along_x = device(y, 1 - x, z, c)
+        self.along_y = device(1 - y, x, z, c)
+        self.across = device(1 - y, 1 - x, z, c)
+        self.along_z = [device(y, x, (z + k) % 4, c) for k in (1, 2, 3)]
+        self.send_sem, self.recv_sem, self.count, self.made = send_sem, recv_sem, 0, []
+
+    def greet(self):
+        barrier = pltpu.get_barrier_semaphore()
+        peers = [self.sibling, self.along_x, self.along_y, self.across] + self.along_z
+        for peer in peers:
+            pl.semaphore_signal(barrier, inc=1, device_id=peer, device_id_type=MESH)
+        pl.semaphore_wait(barrier, len(peers))
+
+    def plan(self, source, target, peer):
+        number = self.count
+        self.count += 1
+        copy = pltpu.make_async_remote_copy(
+            src_ref=source,
+            dst_ref=target,
+            send_sem=self.send_sem.at[number],
+            recv_sem=self.recv_sem.at[number],
+            device_id=peer,
+            device_id_type=MESH,
+        )
+        self.made.append(copy)
+        return copy
+
+    def drain(self):
+        for copy in self.made:
+            copy.wait_send()
+
+
+class Stage:
+    def __init__(self, links, moves):
+        self.copies = [links.plan(*move) for move in moves]
+
+    def start(self):
+        for copy in self.copies:
+            copy.start()
+
+    def wait(self):
+        for copy in self.copies:
+            copy.wait_recv()
+
+
+def at_slots(slot, events):
+    for number, event in enumerate(events):
+        pl.when(slot == number)(event)
+
+
+def front_kernel(scaling, *refs):
+    (live_ref, normal, tile, qkv_shard, out_shard, up_shard, down_shard) = refs[:7]
+    (attended, heads_ref, logsum, rows_ref, gains_ref, qkv, full_out, up, down) = refs[7:16]
+    tiles, staged, send_sem, recv_sem, local_sem = refs[16:]
+    links = Links(send_sem, recv_sem)
+    y, x, z, c = links.y, links.x, links.z, links.c
+    h = y * 2 + x
+    rows = normal.shape[0]
+    wide = qkv.shape[-1]
+    narrow = staged.shape[1]
+    heads = narrow // DH
+    half_ff = up.shape[-1] // 2
+    slot_rows = rows * 4
+    plane = [(links.across, 3 - h, 3), (links.along_x, y * 2 + 1 - x, 1), (links.along_y, (1 - y) * 2 + x, 2)]
+
+    def columns(start, size):
+        return pl.ds(pl.multiple_of(start, 128), size)
+
+    local = [
+        pltpu.make_async_copy(tile, tiles.at[y, x, z, c], local_sem.at[0]),
+        pltpu.make_async_copy(qkv_shard.at[:, columns(h * wide, wide)], qkv.at[y, x, z, c], local_sem.at[1]),
+        pltpu.make_async_copy(out_shard, full_out.at[y, x, z, c], local_sem.at[2]),
+        pltpu.make_async_copy(down_shard, down.at[y, z, c], local_sem.at[3]),
+    ] + [
+        pltpu.make_async_copy(
+            up_shard.at[:, columns(k * 2 * half_ff + x * half_ff, half_ff)],
+            up.at[y, x, z, c, :, k * half_ff : (k + 1) * half_ff],
+            local_sem.at[4 + k],
+        )
+        for k in range(2)
+    ]
+    for copy in local:
+        copy.start()
+    gain_core = Stage(links, [(tile, tiles.at[y, x, z, c], links.sibling)])
+    gain_z = Stage(links, [(tiles.at[y, x, z], tiles.at[y, x, z], peer) for peer in links.along_z])
+    gain_plane = Stage(links, [(tiles.at[y, x], tiles.at[y, x], peer) for peer, _, _ in plane])
+    qkv_plane = Stage(
+        links, [(qkv_shard.at[:, columns(p * wide, wide)], qkv.at[y, x, z, c], peer) for peer, p, _ in plane]
+    )
+    qkv_z = Stage(links, [(qkv.at[:, :, z, c], qkv.at[:, :, z, c], peer) for peer in links.along_z])
+    qkv_core = Stage(links, [(qkv.at[:, :, :, c], qkv.at[:, :, :, c], links.sibling)])
+    up_x = [
+        Stage(
+            links,
+            [
+                (
+                    up_shard.at[:, columns(k * 2 * half_ff + (1 - x) * half_ff, half_ff)],
+                    up.at[y, x, z, c, :, k * half_ff : (k + 1) * half_ff],
+                    links.along_x,
+                )
+            ],
+        )
+        for k in range(2)
+    ]
+
+    def up_part(k, *index):
+        return up.at[(*index, slice(None), slice(k * half_ff, (k + 1) * half_ff))]
+
+    up_z = [
+        Stage(links, [(up_part(k, y, slice(None), z, c),) * 2 + (peer,) for peer in links.along_z]) for k in range(2)
+    ]
+    up_y = [
+        Stage(links, [(up_part(k, y, slice(None), slice(None), c),) * 2 + (links.along_y,)]) for k in range(2)
+    ]
+    up_core = [
+        Stage(links, [(up_part(k, slice(None), slice(None), slice(None), c),) * 2 + (links.sibling,)])
+        for k in range(2)
+    ]
+    down_z = Stage(links, [(down_shard, down.at[y, z, c], peer) for peer in links.along_z])
+    down_y = Stage(links, [(down.at[y, :, c], down.at[y, :, c], links.along_y)])
+    down_core = Stage(links, [(down.at[:, :, c], down.at[:, :, c], links.sibling)])
+    out_z = Stage(links, [(out_shard, full_out.at[y, x, z, c], peer) for peer in links.along_z])
+    out_y = Stage(links, [(full_out.at[y, x, :, c], full_out.at[y, x, :, c], links.along_y)])
+    out_x = Stage(links, [(full_out.at[:, x, :, c], full_out.at[:, x, :, c], links.along_x)])
+    out_core = Stage(links, [(full_out.at[:, :, :, c], full_out.at[:, :, :, c], links.sibling)])
+
+    def strip(p, low, high):
+        return rows_ref.at[p, low:high]
+
+    middle = rows // 2
+    rows_x = [
+        Stage(links, [(strip(h, low, high), strip(h, low, high), links.along_x)])
+        for low, high in ((0, middle), (middle, rows))
+    ]
+    rows_y = [
+        Stage(links, [(strip(h, low, high), strip(h, low, high), links.along_y)])
+        for low, high in ((middle, rows), (0, middle))
+    ]
+    _, at_x, _ = plane[1]
+    _, at_y, _ = plane[2]
+    relay_y = Stage(links, [(strip(at_x, 0, middle), strip(at_x, 0, middle), links.along_y)])
+    relay_x = Stage(links, [(strip(at_y, middle, rows), strip(at_y, middle, rows), links.along_x)])
+
+    links.greet()
+    gain_core.start()
+    qkv_plane.start()
+    up_x[0].start()
+    up_x[1].start()
+    local[0].wait()
+    gain_core.wait()
+    gain_z.start()
+    out_z.start()
+    gain_z.wait()
+    gain_plane.start()
+    local[1].wait()
+    qkv_plane.wait()
+    qkv_z.start()
+    down_z.start()
+    gain_plane.wait()
+    for j in range(8):
+        piece = tiles[j // 4, j // 2 % 2, (j % 2) * 2, 0].astype(jnp.float32)
+        for i in range(1, 4):
+            piece = piece + tiles[j // 4, j // 2 % 2, (j % 2) * 2 + i // 2, i % 2].astype(jnp.float32)
+        gains_ref[:, j * 128 : (j + 1) * 128] = piece[0:8]
+    rows_ref[h] = (normal[...] * gains_ref[0:1, :]).astype(jnp.bfloat16)
+    for stage in (rows_x[0], rows_y[0], rows_x[1], rows_y[1]):
+        stage.start()
+    local[4].wait()
+    local[5].wait()
+    for k in range(2):
+        up_x[k].wait()
+        up_z[k].start()
+    rows_x[0].wait()
+    relay_y.start()
+    rows_y[0].wait()
+    relay_x.start()
+    local[2].wait()
+    out_z.wait()
+    out_y.start()
+    qkv_z.wait()
+    qkv_core.start()
+    qkv_core.wait()
+
+    def project(p):
+        weight = qkv[...].reshape(rows * 4, wide)
+        piece = jnp.dot(rows_ref[p], weight, preferred_element_type=jnp.float32).astype(jnp.bfloat16)
+        at = pl.ds(pl.multiple_of(p * rows, rows), rows)
+        for number in range(3 * heads):
+            heads_ref[number, at, :] = piece[:, number * DH : (number + 1) * DH]
+
+    project(h)
+    rows_x[1].wait()
+    project(at_x)
+    rows_y[1].wait()
+    project(at_y)
+    relay_y.wait()
+    relay_x.wait()
+    project(3 - h)
+
+    live = live_ref[0]
+    key_live = lax.broadcasted_iota(jnp.int32, (slot_rows, 1), 0) < live
+
+    def back(rel):
+        peer = h + (rel % 2) * (1 - 2 * x) + (rel // 2) * (2 - 4 * y)
+        return pltpu.make_async_remote_copy(
+            src_ref=staged.at[pl.ds(pl.multiple_of(peer * rows, rows), rows), :],
+            dst_ref=attended.at[:, columns(h * narrow, narrow)],
+            send_sem=send_sem.at[links.count - 1 + rel],
+            recv_sem=recv_sem.at[links.count - 1 + rel],
+            device_id=(peer, z * 2 + c),
+            device_id_type=MESH,
+        )
+
+    def then(wait, start, extra=None):
+        def run():
+            if extra is not None:
+                extra.wait()
+            wait.wait()
+            start.start()
+
+        return run
+
+    def nothing():
+        pass
+
+    events = [
+        then(down_z, down_y, local[3]),
+        nothing,
+        nothing,
+        then(out_y, out_x),
+        nothing,
+        nothing,
+        nothing,
+        then(up_z[0], up_y[0]),
+        nothing,
+        then(out_x, out_core),
+        nothing,
+        nothing,
+        nothing,
+        then(up_z[1], up_y[1]),
+        nothing,
+        then(down_y, down_core),
+    ]
+
+    def tile_body(slot, carry):
+        turn, number = slot // 4, slot % 4
+        rel = 3 - turn
+        peer = h + (rel % 2) * (1 - 2 * x) + (rel // 2) * (2 - 4 * y)
+        at = pl.ds(pl.multiple_of(peer * rows, rows), rows)
+        at_slots(slot, events)
+        queries = heads_ref[3 * number, at, :]
+        keys = heads_ref[3 * number + 1]
+        values = heads_ref[3 * number + 2]
+        scores = lax.dot_general(keys, queries, (((1,), (1,)), ((), ())), preferred_element_type=jnp.float32)
+        scores = jnp.where(key_live, scores * (scaling * LOG2E), -1e30)
+        highest = jnp.max(scores, axis=0, keepdims=True)
+        raw = jnp.exp2(scores - highest)
+        totals = jnp.sum(raw, axis=0, keepdims=True)
+        weights = (raw * (1.0 / totals)).astype(jnp.bfloat16)
+        mixed = lax.dot_general(
+            values, weights, (((0,), (0,)), ((), ())), preferred_element_type=jnp.float32
+        )
+        mixed = mixed.T.astype(jnp.bfloat16)
+        for which in range(4):
+
+            @pl.when(number == which)
+            def _(which=which):
+                staged[at, which * DH : (which + 1) * DH] = mixed
+
+        logsum[number, :, at] = highest + jnp.log2(totals)
+
+        @pl.when((number == 3) & (rel > 0))
+        def _():
+            back(rel).start()
+
+        return carry
+
+    lax.fori_loop(0, SLOTS, tile_body, 0)
+    own = pltpu.make_async_copy(
+        staged.at[pl.ds(pl.multiple_of(h * rows, rows), rows), :],
+        attended.at[:, columns(h * narrow, narrow)],
+        local_sem.at[6],
+    )
+    own.start()
+    up_y[0].wait()
+    up_core[0].start()
+    for rel in (3, 2, 1):
+        back(rel).wait()
+    up_y[1].wait()
+    up_core[1].start()
+    for stage in (down_core, out_core, up_core[0], up_core[1]):
+        stage.wait()
+    own.wait()
+    links.drain()
+
+
+def front(live, normal, tile, w_qkv, w_out, w_up, w_down, scaling):
+    rows, features = normal.shape
+    vmem, hbm = pl.BlockSpec(memory_space=pltpu.VMEM), pl.BlockSpec(memory_space=pl.ANY)
+    wide = w_qkv.shape[1] // 4
+    heads = wide // (3 * DH)
+    low = jnp.bfloat16
+
+    def full(rows_of, columns_of):
+        return jax.ShapeDtypeStruct((2, 2, 4, 2, rows_of, columns_of), low)
+
+    return pl.pallas_call(
+        partial(front_kernel, scaling),
+        out_shape=[
+            jax.ShapeDtypeStruct((rows, features), low),
+            jax.ShapeDtypeStruct((3 * heads, 4 * rows, DH), low),
+            jax.ShapeDtypeStruct((heads, 1, 4 * rows), jnp.float32),
+            jax.ShapeDtypeStruct((4, rows, features), low),
+            jax.ShapeDtypeStruct((8, features), jnp.float32),
+            full(w_qkv.shape[0], wide),
+            full(*w_out.shape),
+            full(w_up.shape[0], w_up.shape[1] // 2),
+            jax.ShapeDtypeStruct((2, 4, 2) + w_down.shape, low),
+        ],
+        in_specs=[pl.BlockSpec(memory_space=pltpu.SMEM), vmem, vmem] + [hbm] * 4,
+        out_specs=[vmem] * 6 + [hbm] * 3,
+        scratch_shapes=[
+            pltpu.VMEM((2, 2, 4, 2) + tile.shape, low),
+            pltpu.VMEM((4 * rows, wide // 3), low),
+            pltpu.SemaphoreType.DMA((64,)),
+            pltpu.SemaphoreType.DMA((64,)),
+            pltpu.SemaphoreType.DMA((7,)),
+        ],
+        compiler_params=pltpu.CompilerParams(
+            collective_id=1, has_side_effects=True, vmem_limit_bytes=40 * 2**20
+        ),
+        name="front",
+    )(live, normal, tile, w_qkv, w_out, w_up, w_down)
+
+
+class Sum:
+    def __init__(self, links, partial_ref, total, sib, one, two, three, local, kind):
+        y, x, z, c = links.y, links.x, links.z, links.c
+        self.links, self.total, self.sib, self.one, self.two, self.three = links, total, sib, one, two, three
+        self.kind = kind
+        lead = (slice(None),) * (len(total.shape) - 2)
+        self.local = pltpu.make_async_copy(partial_ref.at[(*lead, c)], total, local)
+        self.core = Stage(links, [(partial_ref.at[(*lead, 1 - c)], sib, links.sibling)])
+        if kind == "up":
+            self.first = Stage(links, [(total.at[1 - y], one, links.along_y)])
+            self.second = Stage(
+                links,
+                [(total.at[y, :, (z + k) % 4], two.at[k - 1], links.along_z[k - 1]) for k in (1, 2, 3)],
+            )
+            self.third = Stage(links, [(total.at[y, 1 - x, z], three, links.along_x)])
+        elif kind == "down":
+            self.first = Stage(links, [(total.at[1 - y], one, links.along_y)])
+            self.second = Stage(
+                links, [(total.at[y, (z + k) % 4], two.at[k - 1], links.along_z[k - 1]) for k in (1, 2, 3)]
+            )
+        elif kind == "all":
+            self.first = Stage(links, [(total.at[:, 1 - x], one, links.along_x)])
+            self.second = Stage(links, [(total.at[1 - y, x], two, links.along_y)])
+            self.third = Stage(
+                links,
+                [(total.at[y, x, (z + k) % 4], three.at[k - 1], links.along_z[k - 1]) for k in (1, 2, 3)],
+            )
+
+    def begin(self):
+        self.core.start()
+        self.local.start()
+
+    def add(self, pairs, count):
+        total = self.total
+
+        def body(i, carry):
+            index, extra = pairs(i)
+            total[index] = total[index] + extra
+            return carry
+
+        lax.fori_loop(0, count, body, 0)
+
+    def run_first(self):
+        self.local.wait()
+        self.core.wait()
+        sib = self.sib
+        if self.kind == "down":
+            self.add(lambda i: ((i // 4, i % 4), sib[i // 4, i % 4]), 8)
+        else:
+            self.add(lambda i: ((i // 8, i // 4 % 2, i % 4), sib[i // 8, i // 4 % 2, i % 4]), 16)
+        self.first.start()
+
+    def run_second(self):
+        self.first.wait()
+        y, x, one = self.links.y, self.links.x, self.one
+        if self.kind == "up":
+            self.add(lambda i: ((y, i // 4, i % 4), one[i // 4, i % 4]), 8)
+        elif self.kind == "down":
+            self.add(lambda i: ((y, i), one[i]), 4)
+        else:
+            self.add(lambda i: ((i // 4, x, i % 4), one[i // 4, i % 4]), 8)
+        self.second.start()
+
+    def run_third(self):
+        self.second.wait()
+        y, x, z, two = self.links.y, self.links.x, self.links.z, self.two
+        if self.kind == "up":
+            self.add(lambda i: ((y, i, z), two[0, i] + two[1, i] + two[2, i]), 2)
+        else:
+            self.add(lambda i: ((y, x, i), two[i]), 4)
+        self.third.start()
+
+    def finish(self, out):
+        y, x, z = self.links.y, self.links.x, self.links.z
+        if self.kind == "up":
+            self.third.wait()
+            half = self.total.shape[-1] // 2
+            mine = self.total[y, x, z]
+            theirs = self.three[...]
+            for k in range(2):
+                at = k * 2 * half
+                for low, part in ((0, mine), (1, theirs)):
+                    start = at + (x if low == 0 else 1 - x) * half
+                    out[:, pl.ds(pl.multiple_of(start, 128), half)] = part[
+                        :, k * half : (k + 1) * half
+                    ].astype(jnp.float32)
+            return
+        stage, got = (self.second, self.two) if self.kind == "down" else (self.third, self.three)
+        stage.wait()
+        mine = self.total[y, z] if self.kind == "down" else self.total[y, x, z]
+        value = mine.astype(jnp.float32)
+        for k in range(3):
+            value = value + got[k].astype(jnp.float32)
+        out[...] = value
+
+
+def rear_kernel(scaling, *refs):
+    live_ref, d_rows, heads_ref, logsum, rows_ref, qkv, small_ref = refs[:7]
+    partials = refs[7:12]
+    d_normed, g_qkv, outs, small_out = refs[12], refs[13], refs[14:19], refs[19]
+    at = 20
+    d_out, d_heads, d_spread, grad_keys, grad_values = refs[at : at + 5]
+    d_sent, d_got, q_part, q_sib, q_z, q_plane = refs[at + 5 : at + 11]
+    small_own, small_got, send_sem, recv_sem, local_sem = refs[at + 11 : at + 16]
+    scratch = refs[at + 16 :]
+    links = Links(send_sem, recv_sem)
+    y, x, z, c = links.y, links.x, links.z, links.c
+    h = y * 2 + x
+    rows, features = d_rows.shape
+    slot_rows = rows * 4
+    narrow = d_out.shape[1]
+    heads = narrow // DH
+    wide = 3 * narrow
+    plane = [(links.across, 3 - h, 3), (links.along_x, y * 2 + 1 - x, 1), (links.along_y, (1 - y) * 2 + x, 2)]
+
+    def columns(start, size):
+        return pl.ds(pl.multiple_of(start, 128), size)
+
+    def block(p):
+        return pl.ds(pl.multiple_of(p * rows, rows), rows)
+
+    spread_out = Stage(
+        links, [(d_rows.at[:, columns(p * narrow, narrow)], d_out.at[block(h), :], peer) for peer, p, _ in plane]
+    )
+    own = pltpu.make_async_copy(d_rows.at[:, columns(h * narrow, narrow)], d_out.at[block(h), :], local_sem.at[0])
+    kinds = ("up", "down", "all", "all", "all")
+    sums = [
+        Sum(links, partials[i], *scratch[5 * i : 5 * i + 5], local_sem.at[1 + i], kinds[i]) for i in range(5)
+    ]
+    back = [Stage(links, [(d_sent.at[rel - 1], d_got.at[rel - 1], peer)]) for peer, _, rel in plane]
+    q_core = Stage(links, [(q_part.at[:, :, :, 1 - c], q_sib, links.sibling)])
+    q_along = Stage(
+        links,
+        [(q_part.at[:, :, (z + k) % 4, c], q_z.at[k - 1], links.along_z[k - 1]) for k in (1, 2, 3)],
+    )
+    q_across = Stage(
+        links, [(q_part.at[p // 2, p % 2, z, c], q_plane.at[h], peer) for peer, p, _ in plane]
+    )
+    small_core = Stage(links, [(small_own.at[0], small_got.at[0], links.sibling)])
+    small_x = Stage(links, [(small_own.at[1], small_got.at[1], links.along_x)])
+    small_y = Stage(links, [(small_own.at[2], small_got.at[2], links.along_y)])
+    small_z = Stage(links, [(small_own.at[3], small_got.at[3 + z], peer) for peer in links.along_z])
+
+    links.greet()
+    spread_out.start()
+    own.start()
+    for entry in sums:
+        entry.begin()
+    small_own[0] = small_ref[...]
+    small_core.start()
+    own.wait()
+    spread_out.wait()
+    live = live_ref[0]
+    key_live = lax.broadcasted_iota(jnp.int32, (slot_rows, 1), 0) < live
+    up, down, out, patch, classes = sums
+
+    def small_step(stage, number, following):
+        def run():
+            stage.wait()
+            small_own[number + 1] = small_own[number] + small_got[number]
+            if number == 2:
+                small_got[3 + z] = small_own[3]
+            following.start()
+
+        return run
+
+    def nothing():
+        pass
+
+    events = [
+        up.run_first,
+        patch.run_first,
+        down.run_first,
+        small_step(small_core, 0, small_x),
+        classes.run_first,
+        out.run_first,
+        nothing,
+        small_step(small_x, 1, small_y),
+        patch.run_second,
+        nothing,
+        small_step(small_y, 2, small_z),
+        nothing,
+        up.run_second,
+        nothing,
+        classes.run_second,
+        nothing,
+    ]
+
+    def tile_body(slot, carry):
+        number, turn = slot // 4, slot % 4
+        at_slots(slot, events)
+        at = block(turn)
+
+        @pl.when(turn == 0)
+        def _():
+            grad_keys[...] = jnp.zeros_like(grad_keys)
+            grad_values[...] = jnp.zeros_like(grad_values)
+
+        queries = heads_ref[3 * number, at, :]
+        keys = heads_ref[3 * number + 1]
+        values = heads_ref[3 * number + 2]
+        grads = d_heads[number, at, :]
+        scores = lax.dot_general(keys, queries, (((1,), (1,)), ((), ())), preferred_element_type=jnp.float32)
+        powers = scores * (scaling * LOG2E) - logsum[number, :, at]
+        weights = jnp.where(key_live, jnp.exp2(powers), 0.0)
+        grad_values[...] += jnp.dot(weights.astype(jnp.bfloat16), grads, preferred_element_type=jnp.float32)
+        grad_weights = lax.dot_general(
+            values, grads, (((1,), (1,)), ((), ())), preferred_element_type=jnp.float32
+        )
+        deltas = jnp.sum(grad_weights * weights, axis=0, keepdims=True)
+        grad_scores = (weights * (grad_weights - deltas)).astype(jnp.bfloat16)
+        grad_keys[...] += jnp.dot(grad_scores, queries, preferred_element_type=jnp.float32)
+        grad_queries = lax.dot_general(
+            keys, grad_scores, (((0,), (0,)), ((), ())), preferred_element_type=jnp.float32
+        )
+        d_heads[4 + 3 * number, at, :] = (grad_queries.T * scaling).astype(jnp.bfloat16)
+
+        @pl.when(turn == 3)
+        def _():
+            d_heads[5 + 3 * number] = (grad_keys[...] * scaling).astype(jnp.bfloat16)
+            d_heads[6 + 3 * number] = grad_values[...].astype(jnp.bfloat16)
+
+        return carry
+
+    for number in range(heads):
+        d_heads[number] = d_out[:, number * DH : (number + 1) * DH]
+    lax.fori_loop(0, SLOTS, tile_body, 0)
+    for number in range(3 * heads):
+        d_spread[:, number * DH : (number + 1) * DH] = d_heads[4 + number]
+    per = features // 4
+    for j in range(4):
+        left = jnp.concatenate([rows_ref[p, :, j * per : (j + 1) * per] for p in range(4)], axis=0)
+        piece = lax.dot_general(
+            left, d_spread[...], (((0,), (0,)), ((), ())), preferred_element_type=jnp.float32
+        ).astype(jnp.bfloat16)
+        q_part[j // 2, j % 2] = piece.reshape(4, 2, per // 8, wide)
+    q_core.start()
+    weight = qkv[...].reshape(features, wide)
+    for (_, p, rel), stage in zip(plane, back):
+        piece = lax.dot_general(
+            d_spread[block(p), :], weight, (((1,), (1,)), ((), ())), preferred_element_type=jnp.float32
+        )
+        d_sent[rel - 1] = piece.astype(jnp.bfloat16)
+        stage.start()
+    q_core.wait()
+
+    def add_sib(i, carry):
+        index = (i // 8, i // 4 % 2, i % 4)
+        q_part[(*index, c)] = q_part[(*index, c)] + q_sib[index]
+        return carry
+
+    lax.fori_loop(0, 16, add_sib, 0)
+    q_along.start()
+    d_normed[...] = lax.dot_general(
+        d_spread[block(h), :], weight, (((1,), (1,)), ((), ())), preferred_element_type=jnp.float32
+    )
+    down.run_second()
+    out.run_second()
+    patch.run_third()
+    up.run_third()
+    classes.run_third()
+    out.run_third()
+    q_along.wait()
+
+    def add_z(i, carry):
+        index = (i // 2, i % 2)
+        q_part[(*index, z, c)] = q_part[(*index, z, c)] + (q_z[(0, *index)] + q_z[(1, *index)] + q_z[(2, *index)])
+        return carry
+
+    lax.fori_loop(0, 4, add_z, 0)
+    q_across.start()
+    small_z.wait()
+    small_out[...] = small_got[3] + small_got[4] + small_got[5] + small_got[6]
+    patch.finish(outs[3])
+    down.finish(outs[1])
+    classes.finish(outs[4])
+    out.finish(outs[2])
+    up.finish(outs[0])
+    q_across.wait()
+    g_qkv[:, columns(h * wide, wide)] = q_part[y, x, z, c].astype(jnp.float32)
+    for _, p, _ in plane:
+        g_qkv[:, columns(p * wide, wide)] = q_plane[p].astype(jnp.float32)
+    for stage in back:
+        stage.wait()
+    d_normed[...] = d_normed[...] + (
+        d_got[0].astype(jnp.float32) + d_got[1].astype(jnp.float32) + d_got[2].astype(jnp.float32)
+    )
+    links.drain()
+
+
+def rear(live, d_rows, heads_qkv, logsum, rows_all, qkv, small, partials, scaling):
+    rows, features = d_rows.shape
+    slot_rows = 4 * rows
+    narrow = features // 4
+    heads = narrow // DH
+    wide = 3 * narrow
+    vmem, hbm = pl.BlockSpec(memory_space=pltpu.VMEM), pl.BlockSpec(memory_space=pl.ANY)
+    low = jnp.bfloat16
+    up, down, *rest = [a.shape[-2:] for a in partials]
+    shard = (features // 32, wide)
+    buffers = [
+        (2, 2, 4) + up,
+        (2, 2, 4) + up,
+        (2, 4) + up,
+        (3, 2) + up,
+        up,
+        (2, 4) + down,
+        (2, 4) + down,
+        (4,) + down,
+        (3,) + down,
+        (8, 128),
+    ]
+    for shape in rest:
+        buffers += [(2, 2, 4) + shape, (2, 2, 4) + shape, (2, 4) + shape, (4,) + shape, (3,) + shape]
+    single = jnp.float32
+    return pl.pallas_call(
+        partial(rear_kernel, scaling),
+        out_shape=[
+            jax.ShapeDtypeStruct((rows, features), single),
+            jax.ShapeDtypeStruct((features // 32, 4 * wide), single),
+            jax.ShapeDtypeStruct((up[0], 2 * up[1]), single),
+            jax.ShapeDtypeStruct(down, single),
+        ]
+        + [jax.ShapeDtypeStruct(shape, single) for shape in rest]
+        + [jax.ShapeDtypeStruct(small.shape, single)],
+        in_specs=[pl.BlockSpec(memory_space=pltpu.SMEM)] + [vmem] * 6 + [hbm] * 5,
+        out_specs=[vmem] * 8,
+        scratch_shapes=[
+            pltpu.VMEM((slot_rows, narrow), low),
+            pltpu.VMEM((4 * heads, slot_rows, DH), low),
+            pltpu.VMEM((slot_rows, wide), low),
+            pltpu.VMEM((slot_rows, DH), single),
+            pltpu.VMEM((slot_rows, DH), single),
+            pltpu.VMEM((3, rows, features), low),
+            pltpu.VMEM((3, rows, features), low),
+            pltpu.VMEM((2, 2, 4, 2) + shard, low),
+            pltpu.VMEM((2, 2, 4) + shard, low),
+            pltpu.VMEM((3, 2, 2) + shard, low),
+            pltpu.VMEM((4,) + shard, low),
+            pltpu.VMEM((4,) + small.shape, single),
+            pltpu.VMEM((7,) + small.shape, single),
+            pltpu.SemaphoreType.DMA((64,)),
+            pltpu.SemaphoreType.DMA((64,)),
+            pltpu.SemaphoreType.DMA((6,)),
+        ]
+        + [pltpu.VMEM(shape, low) for shape in buffers],
+        compiler_params=pltpu.CompilerParams(
+            collective_id=2, has_side_effects=True, vmem_limit_bytes=58 * 2**20
+        ),
+        name="rear",
+    )(live, d_rows, heads_qkv, logsum, rows_all, qkv, small, *partials)
+
+
+def hop(value, pairs):
+    return lax.ppermute(value, "head", pairs)
+
+
+def swap(value):
+    return lax.ppermute(value, "head", [(0, 1), (1, 0), (2, 3), (3, 2)])
+
+
+def matmul(left, right):
+    return jnp.dot(left, right, preferred_element_type=jnp.float32)
+
+
+def matmul_nt(left, right):
+    return lax.dot_general(left, right, (((1,), (1,)), ((), ())), preferred_element_type=jnp.float32)
+
+
+def matmul_tn(left, right):
+    return lax.dot_general(left, right, (((0,), (0,)), ((), ())), preferred_element_type=jnp.float32)
+
+
+def body_planned(
+    tokens,
+    patch_counts,
+    w_qkv,
+    w_out,
+    w_up,
+    w_down,
+    w_patch,
+    w_class,
+    norm_gains,
+    mask_norm,
+    grad_masks,
+):
+    low = jnp.bfloat16
+    h, s = lax.axis_index("head"), lax.axis_index("seq")
+    tokens, grad_masks = tokens[0], grad_masks[0]
+    row_count = tokens.shape[0]
+    late = lax.all_gather(jnp.concatenate([w_patch, w_class], axis=1), ("head", "seq"), axis=0, tiled=True)
+    full_patch, full_class = late[:, :1024], late[:, 1024:]
+    tile = lax.dynamic_update_slice(jnp.zeros((16, 128), low), norm_gains, (0, (s % 4) * 32))
+    position = h * row_count + jnp.arange(row_count, dtype=jnp.int32)
+    live = CLS + patch_counts
+    patch_rows = ((position >= CLS) & (position < live[0])).astype(jnp.float32)[:, None]
+    root_flag = (h == 0).astype(jnp.float32)
+    scaling = DH ** (-0.5)
+
+    normal_one, inverse_one = standardize(tokens)
+    attended, heads_qkv, logsum, rows_all, gains, qkv, full_out, half_up, half_down = front(
+        live, normal_one, tile, w_qkv, w_out, w_up, w_down, scaling
+    )
+    full_out = full_out.reshape(1024, 1024)
+    half_up = half_up.reshape(1024, -1)
+    half_down = half_down.reshape(-1, 1024)
+    gain_one, gain_two = gains[0], gains[1]
+    second = tokens + matmul(attended, full_out)
+    normal_two, inverse_two = standardize(second)
+    normed_two = (normal_two * gain_two).astype(low)
+    normed_beside = swap(normed_two)
+    gelu_exact = partial(jax.nn.gelu, approximate=False)
+    hidden = matmul(normed_two, half_up)
+    active = gelu_exact(hidden).astype(low)
+    hidden_beside = matmul(normed_beside, half_up)
+    active_beside = gelu_exact(hidden_beside).astype(low)
+    from_beside = swap(matmul(active_beside, half_down).astype(low))
+    residual = second + (matmul(active, half_down) + from_beside.astype(jnp.float32))
+    rounded = residual.astype(low)
+    class_rows = rounded[:CLS]
+    class_proj = matmul(class_rows, full_class)
+    class_unit = (class_proj * unit_scale(class_proj)).astype(low)
+    arrived = [hop(class_unit, [(0, rel)]) for rel in (1, 2, 3)]
+    patch_proj = matmul(rounded, full_patch)
+    patch_unit = (patch_proj * unit_scale(patch_proj)).astype(low)
+    classes = jnp.where(h == 0, class_unit, arrived[0] + arrived[1] + arrived[2])
+    products = matmul_nt(patch_unit, classes)
+    normal_mask, inverse_mask = standardize(products)
+    class_masks = (normal_mask * mask_norm[0] + mask_norm[1]) * patch_rows
+    upstream = grad_masks * patch_rows
+    mask_sums = jnp.stack([jnp.sum(upstream * normal_mask, axis=0), jnp.sum(upstream, axis=0)])
+    d_products = standard_back(normal_mask, inverse_mask, upstream * mask_norm[0]).astype(low)
+    class_part = matmul_tn(d_products, patch_unit)
+    class_sent = class_part.astype(low)
+    parts = [hop(class_sent, [(rel, 0)]) for rel in (1, 2, 3)]
+    d_patch_unit = matmul(d_products, classes)
+    d_patch_proj = unit_back(patch_proj, d_patch_unit).astype(low)
+    d_class_unit = class_part + (
+        parts[0].astype(jnp.float32) + parts[1].astype(jnp.float32) + parts[2].astype(jnp.float32)
+    )
+    d_class_proj = (unit_back(class_proj, d_class_unit) * root_flag).astype(low)
+    grad_patch = matmul_tn(rounded, d_patch_proj).astype(low)
+    grad_class = matmul_tn(class_rows, d_class_proj).astype(low)
+    d_residual = matmul_nt(d_patch_proj, full_patch)
+    d_residual = d_residual.at[:CLS].add(matmul_nt(d_class_proj, full_class))
+    d_branch = d_residual.astype(low)
+    branch_beside = swap(d_branch)
+    d_active = matmul_nt(d_branch, half_down)
+    d_hidden = jax.vjp(gelu_exact, hidden)[1](d_active)[0].astype(low)
+    d_active_beside = matmul_nt(branch_beside, half_down)
+    d_hidden_beside = jax.vjp(gelu_exact, hidden_beside)[1](d_active_beside)[0].astype(low)
+    back_beside = swap(matmul_nt(d_hidden_beside, half_up).astype(low))
+    d_normed_two = matmul_nt(d_hidden, half_up) + back_beside.astype(jnp.float32)
+    grad_down = matmul_tn(
+        jnp.concatenate([active, active_beside]), jnp.concatenate([d_branch, branch_beside])
+    ).astype(low)
+    grad_up = matmul_tn(
+        jnp.concatenate([normed_two, normed_beside]), jnp.concatenate([d_hidden, d_hidden_beside])
+    ).astype(low)
+    d_second = d_residual + standard_back(normal_two, inverse_two, d_normed_two * gain_two)
+    d_mix = d_second.astype(low)
+    grad_out = matmul_tn(attended, d_mix).astype(low)
+    d_attended = matmul_nt(d_mix, full_out).astype(low)
+
+    def parted(value):
+        return value.reshape(2, 2, 4, 2, value.shape[0] // 32, value.shape[1])
+
+    partials = (
+        parted(grad_up),
+        grad_down.reshape(2, 4, 2, 128, 1024),
+        parted(grad_out),
+        parted(grad_patch),
+        parted(grad_class),
+    )
+    small = jnp.pad(mask_sums, ((0, 6), (0, 256 - CLS)))
+    d_normed_one, g_qkv, g_up, g_down, g_out, g_patch, g_class, sums = rear(
+        live, d_attended, heads_qkv, logsum, rows_all, qkv, small, partials, scaling
+    )
+    grad_inputs = d_second + standard_back(normal_one, inverse_one, d_normed_one * gain_one)
+    gain_sums = [
+        jnp.sum(weight.astype(jnp.float32) * grad, axis=1) for weight, grad in ((w_qkv, g_qkv), (w_up, g_up))
+    ]
+    return (
+        class_masks[None],
+        grad_inputs[None],
+        g_qkv,
+        g_out,
+        g_up,
+        g_down,
+        g_patch,
+        g_class,
+        jnp.stack(gain_sums) / norm_gains.astype(jnp.float32),
+        sums[0:2, :CLS],
+    )
+
+
 def solution(mesh):
+    planned = dict(mesh.shape) == {"head": 4, "seq": 8}
     return jax.shard_map(
-        body,
+        body_planned if planned else body_general,
         mesh=mesh,
         in_specs=(
             P("seq", "head", None),

time: 1830 us -> 447 us (0.24)
  waiting for transfers between devices: 1360 us -> 45.1 us
  Pallas kernels: 0 us -> 277 us
  matrix products: 182 us -> 57.5 us
  blocking collectives: 105 us -> 0 us
  local copies, waits for them, and re-layouts: 84.2 us -> 15.7 us
  other arithmetic: 63.8 us -> 13.7 us
    reduce_scatter x6 -> x0, waiting for transfers between devices: 961 us -> none  [the longest x1 189 us: body(): lax.psum_scatter(grad_up, ('head', 'seq'), scatter_dimension=0, tiled=True)]
    pallas_call x0 -> x2, Pallas kernels: none -> 277 us  [the longest x1 147 us: rear(): pl.pallas_call(partial(rear_kernel, scaling), out_shape=[jax.ShapeDtypeSt...]
    all_gather x6 -> x1, waiting for transfers between devices: 223 us -> 0.01 us  [body_planned(): lax.all_gather(jnp.concatenate([w_patch, w_class], axis=1), ('head', 'seq...]
    dot_general x77 -> x22, matrix products: 182 us -> 57.5 us  [the longest x8 27.3 us: matmul(): return jnp.dot(left, right, preferred_element_type=jnp.float32)]
    psum x2 -> x0, waiting for transfers between devices: 83.8 us -> none  [the longest x1 43.2 us: spread_2(): return lax.psum(kept, axis)]
    unnamed x16 -> x1, waiting for transfers between devices: 51.3 us -> 0.02 us
    ppermute x0 -> x10, waiting for transfers between devices: none -> 45.1 us  [the longest x4 30 us: swap(): return lax.ppermute(value, 'head', [(0, 1), (1, 0), (2, 3), (3, 2)])]
    all_gather x1 -> x0, blocking collectives: 43.2 us -> none  [body(): lax.all_gather(gains_rows, ('head', 'seq'), axis=0, tiled=True)]
  transfers between devices with their start and end apart: 18 -> 11, of which waited for: 17 -> 8; matrix products, arithmetic and copies ran while one was open for 8% -> 11% of each run, Pallas kernels for 0% -> 30%
where the time goes in v2:
time: 447 us; the launch traced here: 438 us
  Pallas kernels  277 us (62%)
  matrix products  57.5 us (13%)
  waiting for transfers between devices  45.1 us (10%)
  local copies, waits for them, and re-layouts  15.7 us (4%)
  between operations  15.7 us (4%)
  other arithmetic  13.7 us (3%)
  starting transfers between devices  13.6 us (3%)
    pallas_call x1, Pallas kernels, rear(): pl.pallas_call(partial(rear_kernel, scaling), out_shape=[jax.ShapeDtypeSt...  147 us
    pallas_call x1, Pallas kernels, front(): pl.pallas_call(partial(front_kernel, scaling), out_shape=[jax.ShapeDtypeS...  130 us
    ppermute x4, waiting for transfers between devices, swap(): return lax.ppermute(value, 'head', [(0, 1), (1, 0), (2, 3), (3, 2)])  30 us
    dot_general x8, matrix products, matmul(): return jnp.dot(left, right, preferred_element_type=jnp.float32)  27.3 us
    dot_general x6, matrix products, matmul_tn(): lax.dot_general(left, right, (((0,), (0,)), ((), ())), preferred_element_...  15.6 us
    ppermute x6, waiting for transfers between devices, hop(): return lax.ppermute(value, 'head', pairs)  15.1 us
    dot_general x8, matrix products, matmul_nt(): lax.dot_general(left, right, (((1,), (1,)), ((), ())), preferred_element_...  14.6 us
    ppermute x6, starting transfers between devices, hop(): return lax.ppermute(value, 'head', pairs)  10.1 us
  transfers between devices with their start and end apart: 11, of which 8 were waited for; matrix products, arithmetic and copies ran while one was open for 11% of the time, Pallas kernels for 30%

profile of v2, /device:TPU:0, one launch (start us, length us, event | category | flops | bytes accessed | tf_op | source)
XLA Modules:
  0.0 438.0 jit_solution(3938138929956113596)
XLA Ops:
  7.2 1.6 pad_maximum_fusion
  11.0 1.5 dynamic_update_slice.3.refs_2_
  13.0 129.9 %front.1 = (bf16[256,1024]{1,0:T(8,128)(2,1)S(1)}, bf16[12,1024,64]{2,1,0:T(8,128)(2,1)S(1)}, f32[4,1,1024]{2,1,0:T(1,128)S(1)}, bf16[4,256,1024]{2,1,0:T(8,128)...) custom-call(s32[1]{0:T(128)} %add.114.refs_0_, ...), custom_call_target="tpu_custom_call" | custom-call | tf_op jit(solution)/shard_map/front/pallas_call | solution.py:618
  148.4 1.5 collective-permute-start
  149.9 12.8 %collective-permute-done = bf16[256,1024]{1,0:T(8,128)(2,1)S(1)} collective-permute-done((bf16[256,1024]{1,0:T(8,128)(2,1)S(1)}, bf16[256,1024]{1,0:T(8,128)(2,1)S(1)}, u32[]{:S(2)}, u32[]{:S(2)}) %collective-permute-start) | collective-permute-done | bytes 524320 | tf_op jit(solution)/shard_map/ppermute | solution.py:1005
  162.7 6.9 %multiply_convert_fusion = (bf16[256,2048]{1,0:T(8,128)(2,1)S(1)}, f32[256,2048]{1,0:T(8,128)}, f32[256,2048]{1,0:T(8,128)}) fusion(bf16[256,1024]{1,0:T(8,128)(2,1)S(1)} %collective-permute-done, bf16[1024,2048]{1,0:T(8,128)(2,1)S(1)} %bitcast.93), kind=kOutput, calls=%fused_computation.14 | convolution fusion | flops 1107820544 | bytes 9961472 | tf_op jit(solution)/shard_map/dot_general | solution.py:1009
  169.7 2.0 convolution_convert_fusion.7
  173.2 7.4 %multiply_convert_fusion.1 = (bf16[256,2048]{1,0:T(8,128)(2,1)}, f32[256,2048]{1,0:T(8,128)}, f32[256,2048]{1,0:T(8,128)}) fusion(bf16[256,1024]{1,0:T(8,128)(2,1)S(1)} %multiply_convert_fusion.3, bf16[1024,2048]{1,0:T(8,128)(2,1)S(1)} %bitcast.94), kind=kOutput, calls=%fused_computation.27 | convolution fusion | flops 1107820544 | bytes 9961472 | tf_op jit(solution)/shard_map/dot_general | solution.py:1009
  180.7 4.9 %collective-permute-done.1 = bf16[256,1024]{1,0:T(8,128)(2,1)} collective-permute-done((bf16[256,1024]{1,0:T(8,128)(2,1)}, bf16[256,1024]{1,0:T(8,128)(2,1)}, u32[]{:S(2)}, u32[]{:S(2)}) %collective-permute-start.1) | collective-permute-done | bytes 524320 | tf_op jit(solution)/shard_map/ppermute | solution.py:1005
  185.5 5.0 %add_convert_fusion.2 = bf16[256,1024]{1,0:T(8,128)(2,1)} fusion(f32[256,1024]{1,0:T(8,128)} %copy-done.11, bf16[256,1024]{1,0:T(8,128)(2,1)} %collective-permute-done.1, bf16[256,2048]{1,0:T(8,128)(2,1)} %get-tuple-element.76, bf16[2048,1024]{1,0:T(8,128)(2,1)} %bitcast.97), kind=kOutput, calls=%fused_computation.73 | convolution fusion | flops 1074790400 | bytes 7340032 | tf_op jit(solution)/shard_map/dot_general | solution.py:1009
  190.5 2.4 multiply_reduce_fusion.8
  193.0 3.4 collective-permute-start.4
  199.0 2.4 multiply_reduce_fusion.3
  201.4 2.7 collective-permute-done.4
  204.2 4.4 collective-permute-done.2
  210.3 1.6 collective-permute-start.7
  216.9 2.1 convolution_convert_fusion.2
  220.5 6.6 %collective-permute-done.6 = bf16[150,1024]{1,0:T(8,128)(2,1)S(1)} collective-permute-done((bf16[150,1024]{1,0:T(8,128)(2,1)S(1)}, bf16[150,1024]{1,0:T(8,128)(2,1)S(1)}, u32[]{:S(2)}, u32[]{:S(2)}) %collective-permute-start.6) | collective-permute-done | bytes 307232 | tf_op jit(solution)/shard_map/ppermute | solution.py:1001
  227.6 2.1 convolution_convert_fusion.4
  229.7 1.7 fusion.26
  231.4 3.2 scatter-add.4
  236.1 5.4 %add_convert_fusion.1 = bf16[256,2048]{1,0:T(8,128)(2,1)S(1)} fusion(f32[256,2048]{1,0:T(8,128)} %get-tuple-element.77, f32[256,2048]{1,0:T(8,128)} %get-tuple-element.86, bf16[256,1024]{1,0:T(8,128)(2,1)S(1)} %convert_element_type.119, bf16[2048,1024]{1,0:T(8,128)(2,1)} %bitcast.98), kind=kOutput, calls=%fused_computation.13 | convolution fusion | flops 1081081856 | bytes 9961472 | tf_op jit(solution)/shard_map/dot_general | solution.py:1013
  241.5 8.4 %collective-permute-done.8 = bf16[256,1024]{1,0:T(8,128)(2,1)S(1)} collective-permute-done((bf16[256,1024]{1,0:T(8,128)(2,1)S(1)}, bf16[256,1024]{1,0:T(8,128)(2,1)S(1)}, u32[]{:S(2)}, u32[]{:S(2)}) %collective-permute-start.8) | collective-permute-done | bytes 524320 | tf_op jit(solution)/shard_map/ppermute | solution.py:1005
  249.9 2.0 add_convert_fusion
  253.7 4.4 convolution_convert_fusion.1
  258.1 4.4 convolution_convert_fusion
  262.5 4.0 collective-permute-done.9
  266.5 1.5 fusion.38
  268.4 1.5 convolution_convert_fusion.5.refs_1_
  270.0 2.3 convolution_convert_fusion.3
  272.3 146.8 %rear.1 = (f32[256,1024]{1,0:T(8,128)}, f32[32,3072]{1,0:T(8,128)}, f32[32,4096]{1,0:T(8,128)}, f32[128,1024]{1,0:T(8,128)}, f32[32,1024]{1,0:T(8,128)}, /*index...) custom-call(s32[1]{0:T(128)} %add.114.refs_0_, bf16[256,1024]{1,0:T(8,128)(2,1)} %convolution_convert_fusion.5.refs_1_, ...), custom_call_target="tpu_custom_call" | custom-call | tf_op jit(solution)/shard_map/rear/pallas_call | solution.py:962
  422.9 1.5 multiply_reduce_fusion.6
  (144 shorter events, 34.1 us)
Async XLA Ops:
  7.2 5.4 %copy-start.8 = (f32[1,256,1024]{2,1,0:T(8,128)S(1)}, f32[1,256,1024]{2,1,0:T(8,128)}, u32[]{:S(2)}) copy-start(f32[1,256,1024]{2,1,0:T(8,128)} %param.13) | copy-start | bytes 3145732
  7.2 183.3 %all-gather.2.cloned.1.call-start = ((), (), s32[]{:S(2)}) async-start(), calls=%async_computation | async-start | bytes 4325376 | tf_op jit(solution)/shard_map/all_gather | solution.py:1037
  12.8 132.0 %copy-start.9 = (f32[1,256,1024]{2,1,0:T(8,128)S(1)}, f32[1,256,1024]{2,1,0:T(8,128)}, u32[]{:S(2)}) copy-start(f32[1,256,1024]{2,1,0:T(8,128)} %param.13) | copy-start | bytes 3145732
  144.8 17.9 %copy-start.29 = (bf16[2,2,4,2,32,2048]{5,4,3,2,1,0:T(8,128)(2,1)S(1)}, bf16[2,2,4,2,32,2048]{5,4,3,2,1,0:T(8,128)(2,1)}, u32[]{:S(2)}) copy-start(bf16[2,2,4,2,32,2048]{5,4,3,2,1,0:T(8,128)(2,1)} %get-tuple-element.42) | copy-start | bytes 12582916
  148.4 24.8 %copy-start.21 = (bf16[256,1024]{1,0:T(8,128)(2,1)}, bf16[256,1024]{1,0:T(8,128)(2,1)S(1)}, u32[]{:S(2)}) copy-start(bf16[256,1024]{1,0:T(8,128)(2,1)S(1)} %multiply_convert_fusion.3) | copy-start | bytes 1572868
  148.4 14.3 %collective-permute-start = (bf16[256,1024]{1,0:T(8,128)(2,1)S(1)}, bf16[256,1024]{1,0:T(8,128)(2,1)S(1)}, u32[]{:S(2)}, u32[]{:S(2)}) collective-permute-start(bf16[256,1024]{1,0:T(8,128)(2,1)S(1)} %multiply_convert_fusion.3), channel_id=1, source_target_pairs={{0,8},{8,0},{16,24},{24,16},{1,9},{9,1},{17,25},{25,17},{2,10},{10... | collective-permute-start | bytes 1572872 | tf_op jit(solution)/shard_map/ppermute | solution.py:1005
  162.7 7.0 %copy-start.33 = (bf16[256,1024]{1,0:T(8,128)(2,1)}, bf16[256,1024]{1,0:T(8,128)(2,1)S(1)}, u32[]{:S(2)}) copy-start(bf16[256,1024]{1,0:T(8,128)(2,1)S(1)} %collective-permute-done) | copy-start | bytes 1572868
  162.7 7.0 %copy-start.31 = (bf16[2,4,2,128,1024]{4,3,2,1,0:T(8,128)(2,1)S(1)}, bf16[2,4,2,128,1024]{4,3,2,1,0:T(8,128)(2,1)}, u32[]{:S(2)}) copy-start(bf16[2,4,2,128,1024]{4,3,2,1,0:T(8,128)(2,1)} %get-tuple-element.43) | copy-start | bytes 12582916
  171.7 8.9 %copy-start.27 = (f32[2,150]{1,0:T(2,128)S(1)}, f32[2,150]{1,0:T(2,128)}, u32[]{:S(2)}) copy-start(f32[2,150]{1,0:T(2,128)} %param.22) | copy-start | bytes 3604
  171.7 13.8 %collective-permute-start.1 = (bf16[256,1024]{1,0:T(8,128)(2,1)}, bf16[256,1024]{1,0:T(8,128)(2,1)}, u32[]{:S(2)}, u32[]{:S(2)}) collective-permute-start(bf16[256,1024]{1,0:T(8,128)(2,1)} %convolution_convert_fusion.7), channel_id=1, source_target_pairs={{0,8},{8,0},{16,24},{24,16},{1,9},{9,1},{17,25},{25,17},{2,10},{10... | collective-permute-start | bytes 1572872 | tf_op jit(solution)/shard_map/ppermute | solution.py:1005
  190.5 8.5 %copy-start.18 = (bf16[256,1024]{1,0:T(8,128)(2,1)S(1)}, bf16[256,1024]{1,0:T(8,128)(2,1)}, u32[]{:S(2)}) copy-start(bf16[256,1024]{1,0:T(8,128)(2,1)} %add_convert_fusion.2) | copy-start | bytes 1572868
  193.0 11.2 %collective-permute-start.4 = (bf16[150,1024]{1,0:T(8,128)(2,1)S(1)}, bf16[150,1024]{1,0:T(8,128)(2,1)S(1)}, u32[]{:S(2)}, u32[]{:S(2)}) collective-permute-start(bf16[150,1024]{1,0:T(8,128)(2,1)S(1)} %multiply_convert_fusion.6), channel_id=1, source_target_pairs={{0,24},{1,25},{2,26},{3,27},{4,28},{5,29},{6,30},{7,31}} | collective-permute-start | bytes 921608 | tf_op jit(solution)/shard_map/ppermute | solution.py:1001
  196.4 7.8 %collective-permute-start.3 = (bf16[150,1024]{1,0:T(8,128)(2,1)S(1)}, bf16[150,1024]{1,0:T(8,128)(2,1)S(1)}, u32[]{:S(2)}, u32[]{:S(2)}) collective-permute-start(bf16[150,1024]{1,0:T(8,128)(2,1)S(1)} %multiply_convert_fusion.6), channel_id=1, source_target_pairs={{0,16},{1,17},{2,18},{3,19},{4,20},{5,21},{6,22},{7,23}} | collective-permute-start | bytes 921608 | tf_op jit(solution)/shard_map/ppermute | solution.py:1001
  197.7 10.8 %collective-permute-start.2 = (bf16[150,1024]{1,0:T(8,128)(2,1)S(1)}, bf16[150,1024]{1,0:T(8,128)(2,1)S(1)}, u32[]{:S(2)}, u32[]{:S(2)}) collective-permute-start(bf16[150,1024]{1,0:T(8,128)(2,1)S(1)} %multiply_convert_fusion.6), channel_id=1, source_target_pairs={{0,8},{1,9},{2,10},{3,11},{4,12},{5,13},{6,14},{7,15}} | collective-permute-start | bytes 921608 | tf_op jit(solution)/shard_map/ppermute | solution.py:1001
  201.4 7.8 %copy-start.20 = (f32[1,256,150]{1,0,2:T(1,128)S(1)}, f32[1,256,150]{1,0,2:T(1,128)}, u32[]{:S(2)}) copy-start(f32[1,256,150]{1,0,2:T(1,128)} %param.23) | copy-start | bytes 460804
  209.9 4.7 %copy-start.19 = (bf16[1024,2048]{1,0:T(8,128)(2,1)S(1)}, bf16[1024,2048]{1,0:T(8,128)(2,1)}, u32[]{:S(2)}) copy-start(bf16[1024,2048]{1,0:T(8,128)(2,1)} %all-gather.2.cloned.1.call-done) | copy-start | bytes 12582916
  210.3 10.2 %collective-permute-start.7 = (bf16[150,1024]{1,0:T(8,128)(2,1)S(1)}, bf16[150,1024]{1,0:T(8,128)(2,1)S(1)}, u32[]{:S(2)}, u32[]{:S(2)}) collective-permute-start(bf16[150,1024]{1,0:T(8,128)(2,1)S(1)} %get-tuple-element.96), channel_id=1, source_target_pairs={{24,0},{25,1},{26,2},{27,3},{28,4},{29,5},{30,6},{31,7}} | collective-permute-start | bytes 921608 | tf_op jit(solution)/shard_map/ppermute | solution.py:1001
  211.8 15.2 %collective-permute-start.6 = (bf16[150,1024]{1,0:T(8,128)(2,1)S(1)}, bf16[150,1024]{1,0:T(8,128)(2,1)S(1)}, u32[]{:S(2)}, u32[]{:S(2)}) collective-permute-start(bf16[150,1024]{1,0:T(8,128)(2,1)S(1)} %get-tuple-element.96), channel_id=1, source_target_pairs={{16,0},{17,1},{18,2},{19,3},{20,4},{21,5},{22,6},{23,7}} | collective-permute-start | bytes 921608 | tf_op jit(solution)/shard_map/ppermute | solution.py:1001
  213.1 13.9 %collective-permute-start.5 = (bf16[150,1024]{1,0:T(8,128)(2,1)S(1)}, bf16[150,1024]{1,0:T(8,128)(2,1)S(1)}, u32[]{:S(2)}, u32[]{:S(2)}) collective-permute-start(bf16[150,1024]{1,0:T(8,128)(2,1)S(1)} %get-tuple-element.96), channel_id=1, source_target_pairs={{8,0},{9,1},{10,2},{11,3},{12,4},{13,5},{14,6},{15,7}} | collective-permute-start | bytes 921608 | tf_op jit(solution)/shard_map/ppermute | solution.py:1001
  215.4 14.3 %copy-start.13 = (f32[256,1024]{1,0:T(8,128)}, f32[256,1024]{1,0:T(8,128)S(1)}, u32[]{:S(2)}) copy-start(f32[256,1024]{1,0:T(8,128)S(1)} %fusion.22) | copy-start | bytes 3145732
  235.9 13.9 %collective-permute-start.8 = (bf16[256,1024]{1,0:T(8,128)(2,1)S(1)}, bf16[256,1024]{1,0:T(8,128)(2,1)S(1)}, u32[]{:S(2)}, u32[]{:S(2)}) collective-permute-start(bf16[256,1024]{1,0:T(8,128)(2,1)S(1)} %convert_element_type.119), channel_id=1, source_target_pairs={{0,8},{8,0},{16,24},{24,16},{1,9},{9,1},{17,25},{25,17},{2,10},{10... | collective-permute-start | bytes 1572872 | tf_op jit(solution)/shard_map/ppermute | solution.py:1005
  236.0 13.8 %copy-start.32 = (bf16[2,4,2,128,1024]{4,3,2,1,0:T(8,128)(2,1)S(1)}, bf16[2,4,2,128,1024]{4,3,2,1,0:T(8,128)(2,1)}, u32[]{:S(2)}) copy-start(bf16[2,4,2,128,1024]{4,3,2,1,0:T(8,128)(2,1)} %get-tuple-element.43) | copy-start | bytes 12582916
  236.0 13.8 %copy-start.38 = (f32[256,2048]{1,0:T(8,128)S(1)}, f32[256,2048]{1,0:T(8,128)}, u32[]{:S(2)}) copy-start(f32[256,2048]{1,0:T(8,128)} %get-tuple-element.75) | copy-start | bytes 6291460
  236.0 13.8 %copy-start.39 = (f32[256,2048]{1,0:T(8,128)S(1)}, f32[256,2048]{1,0:T(8,128)}, u32[]{:S(2)}) copy-start(f32[256,2048]{1,0:T(8,128)} %get-tuple-element.87) | copy-start | bytes 6291460
  253.4 4.7 %copy-start.35 = (bf16[256,2048]{1,0:T(8,128)(2,1)S(1)}, bf16[256,2048]{1,0:T(8,128)(2,1)}, u32[]{:S(2)}) copy-start(bf16[256,2048]{1,0:T(8,128)(2,1)} %get-tuple-element.76) | copy-start | bytes 3145732
  253.4 4.7 %copy-start.37 = (bf16[256,2048]{1,0:T(8,128)(2,1)S(1)}, bf16[256,2048]{1,0:T(8,128)(2,1)}, u32[]{:S(2)}) copy-start(bf16[256,2048]{1,0:T(8,128)(2,1)} %copy-done.36) | copy-start | bytes 3145732
  253.4 13.1 %collective-permute-start.9 = (bf16[256,1024]{1,0:T(8,128)(2,1)S(1)}, bf16[256,1024]{1,0:T(8,128)(2,1)S(1)}, u32[]{:S(2)}, u32[]{:S(2)}) collective-permute-start(bf16[256,1024]{1,0:T(8,128)(2,1)S(1)} %convolution_convert_fusion.6), channel_id=1, source_target_pairs={{0,8},{8,0},{16,24},{24,16},{1,9},{9,1},{17,25},{25,17},{2,10},{10... | collective-permute-start | bytes 1572872 | tf_op jit(solution)/shard_map/ppermute | solution.py:1005
  258.1 8.4 %copy-start.12 = (f32[256,1024]{1,0:T(8,128)S(1)}, f32[256,1024]{1,0:T(8,128)}, u32[]{:S(2)}) copy-start(f32[256,1024]{1,0:T(8,128)} %copy-done.11) | copy-start | bytes 3145732
  262.5 5.5 %copy-start.14 = (f32[256,1024]{1,0:T(8,128)S(1)}, f32[256,1024]{1,0:T(8,128)}, u32[]{:S(2)}) copy-start(f32[256,1024]{1,0:T(8,128)} %scatter-add.4) | copy-start | bytes 3145732
  419.0 3.8 copy-start.10
  419.1 5.4 %copy-start.28 = (bf16[2,32]{1,0:T(2,128)(2,1)S(1)}, bf16[2,32]{1,0:T(2,128)(2,1)}, u32[]{:S(2)}) copy-start(bf16[2,32]{1,0:T(2,128)(2,1)} %param.21) | copy-start | bytes 388
  419.1 5.9 %copy-start.15 = (f32[256,1024]{1,0:T(8,128)S(1)}, f32[256,1024]{1,0:T(8,128)}, u32[]{:S(2)}) copy-start(f32[256,1024]{1,0:T(8,128)} %get-tuple-element.48) | copy-start | bytes 3145732
  (19 other events, 43.4 us)
Sparse Core Ops, SparseCore 0:
  11.6 94.2 all-gather.1
